TPU v7x, 32 devices: a whole 2x2x4 slice. The times are simulated.
32 devices in a mesh: dp: 4 (over x, core), ctx: 8 (over z, y).
Axes of the slice: x: 2, y: 2, z: 4, core: 2. Of those that a mesh axis runs over, the one named last changes fastest.
Arguments:
- merged_grad: bfloat16 [4096, 1792], P(('dp', 'ctx')), may hold values from -6 to 6
- merged_owner: int32 [4096, 1], P(('dp', 'ctx')), may hold values from 0 to 7; in each aligned block of 128 rows (0 to 127, 128 to 255, ...) at most 32 rows name the same one
- merger_pre: bfloat16 [8192, 2560], P(('dp', 'ctx')), may hold values from -6 to 6
- fc2_weight: bfloat16 [2560, 1792], P('ctx'), may hold values from -0.125 to 0.125
- query: bfloat16 [8192, 1280], P(('dp', 'ctx')), may hold values from -32 to 32
- key_states: bfloat16 [8192, 1280], P(('dp', 'ctx')), may hold values from -32 to 32
- value_states: bfloat16 [8192, 1280], P(('dp', 'ctx')), may hold values from -6 to 6
- out_grad: bfloat16 [8192, 1280], P(('dp', 'ctx')), may hold values from -6 to 6
- position: int32 [2, 8192], P(None, ('dp', 'ctx')), may hold values from 0 to 63, as said below
Outputs:
- hidden_grad: bfloat16 [8192, 2560], P(('dp', 'ctx'))
- weight_grad: float32 [2560, 1792], P('ctx', 'dp')
- query_grad: bfloat16 [8192, 1280], P(('dp', 'ctx'))
- key_grad: bfloat16 [8192, 1280], P(('dp', 'ctx'))
- value_grad: bfloat16 [8192, 1280], P(('dp', 'ctx'))
Inputs may be any that keep to these rules, and one draw needn't show every extreme that they name: `merged_owner`: in each device's block of 128 rows no owner is named more than 32 times. `position`: each window of 64 consecutive patches covers an aligned square of 8 by 8 grid positions, row by row.
All inputs are finite; a program needn't handle non-finite values.
Results may differ from a plain program's by a relative error of at most 0.0017.
The roundings to bfloat16 on the way count: a program that leaves them out, or rounds other values in their place, can miss the bound.
Values may be sent and summed in bfloat16 or wider, within the bound.
A program may use at most 128 MiB of HBM per device.

v0:
```python
import functools
import math

import jax
import jax.numpy as jnp
from jax import lax
from jax.experimental import pallas as pl
from jax.experimental.pallas import tpu as pltpu
from jax.sharding import PartitionSpec as P

HEAD = 80
WIN = 64
LANES = 128
F32 = jnp.float32
BF16 = jnp.bfloat16
MESH = pl.DeviceIdType.MESH


def rope_tables(position):
    quarter = HEAD // 4
    freq = 1.0 / 10000.0 ** (jnp.arange(quarter, dtype=F32) * (4.0 / HEAD))
    rows = position[0].astype(F32)[:, None] * freq[None, :]
    cols = position[1].astype(F32)[:, None] * freq[None, :]
    angles = jnp.concatenate([rows, cols], axis=1)
    cosine, sine = jnp.cos(angles), jnp.sin(angles)
    pad = jnp.zeros((angles.shape[0], LANES - HEAD), F32)
    return (
        jnp.concatenate([cosine, cosine, pad], axis=1),
        jnp.concatenate([-sine, sine, pad], axis=1),
    )


def spread(table, width):
    shape = (LANES, width)
    lane = lax.broadcasted_iota(jnp.int32, shape, 1) % HEAD
    pick = (lane == lax.broadcasted_iota(jnp.int32, shape, 0)).astype(F32).astype(BF16)
    high = table.astype(BF16)
    rest = table - high.astype(F32)
    mid = rest.astype(BF16)
    low = (rest - mid.astype(F32)).astype(BF16)
    dot = functools.partial(jnp.dot, preferred_element_type=F32)
    return dot(high, pick) + dot(mid, pick) + dot(low, pick)


def attention_window(w, q_ref, k_ref, v_ref, g_ref, c_ref, s_ref, dq_ref, dk_ref, dv_ref):
    at = pl.ds(pl.multiple_of(w * WIN, WIN), WIN)
    width = q_ref.shape[1]
    heads = width // HEAD
    half = HEAD // 2
    cosine = spread(c_ref[at, :], width)
    sine = spread(s_ref[at, :], width)
    lane = lax.broadcasted_iota(jnp.int32, (WIN, width), 1)
    first = lane % HEAD < half

    def swap(x):
        return jnp.where(first, pltpu.roll(x, width - half, 1), pltpu.roll(x, half, 1))

    def rotated(x):
        return (x * cosine + swap(x) * sine).astype(BF16)

    def unrotated(x):
        return (x * cosine - swap(x) * sine).astype(BF16)

    q = rotated(q_ref[at, :].astype(F32))
    k = rotated(k_ref[at, :].astype(F32))
    v = v_ref[at, :]
    g = g_ref[at, :]
    factor = HEAD ** (-0.5)
    nt = (((1,), (1,)), ((), ()))
    tn = (((0,), (0,)), ((), ()))
    nn = (((1,), (0,)), ((), ()))

    def dot(a, b, dims):
        return lax.dot_general(a, b, dims, preferred_element_type=F32)

    dq, dk, dv = {}, {}, {}

    def add(into, tile, value):
        for i in range(value.shape[1] // LANES):
            part = value[:, i * LANES : (i + 1) * LANES]
            into[tile + i] = into[tile + i] + part if tile + i in into else part

    for head in range(heads):
        tile = head * HEAD // LANES
        end = -(-(head + 1) * HEAD // LANES)
        lo, hi = tile * LANES, end * LANES
        here = lax.broadcasted_iota(jnp.int32, (1, hi - lo), 1) + lo
        mask = ((here >= head * HEAD) & (here < (head + 1) * HEAD)).astype(F32).astype(BF16)
        qm = q[:, lo:hi] * mask
        km = k[:, lo:hi] * mask
        gm = g[:, lo:hi] * mask
        scores = dot(qm, k[:, lo:hi], nt) * factor
        weight = jnp.exp(scores - jnp.max(scores, axis=1, keepdims=True))
        probs = weight * (1.0 / jnp.sum(weight, axis=1, keepdims=True))
        probs_b = probs.astype(BF16)
        prob_grad = dot(gm, v[:, lo:hi], nt)
        delta = jnp.sum(probs_b.astype(F32) * prob_grad, axis=1, keepdims=True)
        score_grad = (probs * (prob_grad - delta)).astype(BF16)
        add(dv, tile, dot(probs_b, gm, tn))
        add(dq, tile, dot(score_grad, km, nn))
        add(dk, tile, dot(score_grad, qm, tn))

    def joined(parts):
        return jnp.concatenate([parts[i] for i in range(width // LANES)], axis=1)

    dq_ref[at, :] = unrotated(joined(dq) * factor)
    dk_ref[at, :] = unrotated(joined(dk) * factor)
    dv_ref[at, :] = joined(dv).astype(BF16)


def fused_kernel(
    owners_count,
    replicas,
    m_ref,
    o_ref,
    p_ref,
    w_ref,
    q_ref,
    k_ref,
    v_ref,
    g_ref,
    c_ref,
    s_ref,
    h_out,
    wg_out,
    dq_ref,
    dk_ref,
    dv_ref,
    mall,
    owners,
    pre_got,
    code,
    act,
    hid,
    hid_out,
    full,
    part,
    part_got,
    m_recv,
    up_sem,
    down_sem,
    side_sem,
    o_send,
    o_recv,
    p_send,
    p_recv,
    h_send,
    h_recv,
    r_send,
    r_recv,
    local_sem,
):
    n = owners_count
    sides = 2
    line = n // sides
    rows_here = m_ref.shape[0]
    mine, slots = pre_got.shape[1:]
    block = sides * rows_here
    blocks = n // sides
    windows = q_ref.shape[0] // WIN
    me = lax.axis_index("ctx")
    rep = lax.axis_index("dp")
    a, b = me // sides, me % sides

    barrier = pltpu.get_barrier_semaphore()
    for r in range(1, n):
        pl.semaphore_signal(barrier, inc=1, device_id={"dp": rep, "ctx": (me + r) % n}, device_id_type=MESH)
    for r in range(1, replicas):
        pl.semaphore_signal(
            barrier, inc=1, device_id={"dp": (rep + r) % replicas, "ctx": me}, device_id_type=MESH
        )
    pl.semaphore_wait(barrier, n - 1 + replicas - 1)

    def send(src, dst, send_sem, recv_sem, ctx=None, dp=None):
        where = {"dp": rep if dp is None else dp, "ctx": me if ctx is None else ctx}
        return pltpu.make_async_remote_copy(
            src_ref=src,
            dst_ref=dst,
            send_sem=send_sem,
            recv_sem=recv_sem,
            device_id=where,
            device_id_type=MESH,
        )

    def owner_copy(r):
        return send(o_ref, owners.at[me], o_send.at[r - 1], o_recv.at[r - 1], ctx=(me + r) % n)

    def pre_copy(r):
        peer = (me + r) % n
        return send(p_ref.at[peer], pre_got.at[me], p_send.at[r - 1], p_recv.at[r - 1], ctx=peer)

    def hidden_copy(r):
        peer = (me + r) % n
        return send(hid_out.at[peer], h_out.at[me], h_send.at[r - 1], h_recv.at[r - 1], ctx=peer)

    def part_copy(r):
        peer = (rep + r) % replicas
        return send(part.at[peer], part_got.at[r - 1], r_send.at[r - 1], r_recv.at[r - 1], dp=peer)

    def up_copy(t, ref):
        return send(ref, mall.at[(a - t) * sides + b], up_sem.at[t], m_recv.at[(a - t) * sides + b], ctx=me + sides)

    def down_copy(t, ref):
        return send(ref, mall.at[(a + t) * sides + b], down_sem.at[t], m_recv.at[(a + t) * sides + b], ctx=me - sides)

    def side_copy(at, ref):
        return send(ref, mall.at[at * sides + b], side_sem.at[at], m_recv.at[at * sides + b], ctx=a * sides + 1 - b)

    def arrived(src):
        send(mall.at[src], mall.at[src], up_sem.at[0], m_recv.at[src], ctx=a * sides + 1 - b).wait_recv()

    for r in range(1, n):
        owner_copy(r).start()

    @pl.when(a + 1 < line)
    def _():
        up_copy(0, m_ref).start()

    @pl.when(a > 0)
    def _():
        down_copy(0, m_ref).start()

    side_copy(a, m_ref).start()
    for r in range(1, n):
        pre_copy(r).start()
    locals_ = [
        pltpu.make_async_copy(m_ref, mall.at[me], local_sem.at[0]),
        pltpu.make_async_copy(o_ref, owners.at[me], local_sem.at[1]),
        pltpu.make_async_copy(p_ref.at[me], pre_got.at[me], local_sem.at[2]),
    ]
    for copy in locals_:
        copy.start()

    def forward(t):
        @pl.when(a - t >= 0)
        def _():
            ref = mall.at[(a - t) * sides + b]
            arrived((a - t) * sides + b)

            @pl.when(a + 1 < line)
            def _():
                up_copy(t, ref).start()

            side_copy(a - t, ref).start()

        @pl.when(a + t < line)
        def _():
            ref = mall.at[(a + t) * sides + b]
            arrived((a + t) * sides + b)

            @pl.when(a > 0)
            def _():
                down_copy(t, ref).start()

            side_copy(a + t, ref).start()

    def with_window(w, carry):
        attention_window(w, q_ref, k_ref, v_ref, g_ref, c_ref, s_ref, dq_ref, dk_ref, dv_ref)

        @pl.when(w + 1 < line)
        def _():
            forward(w + 1)

        return carry

    lax.fori_loop(0, windows, with_window, 0)

    def only_forward(t, carry):
        forward(t)
        return carry

    if windows + 1 < line:
        lax.fori_loop(windows + 1, line, only_forward, 0)

    for copy in locals_:
        copy.wait()
    for r in range(1, n):
        owner_copy(r).wait()

    padded = -(-n // 16) * 16
    earlier = lax.broadcasted_iota(jnp.int32, (rows_here, rows_here), 0) < lax.broadcasted_iota(
        jnp.int32, (rows_here, rows_here), 1
    )
    earlier = earlier.astype(F32).astype(BF16)
    names = lax.broadcasted_iota(jnp.int32, (padded, rows_here), 0)
    base = jnp.zeros((padded, 1), F32)
    for s in range(n):
        onehot = (names == owners[s, 0:1, :]).astype(F32)
        count = jnp.dot(onehot.astype(BF16), earlier, preferred_element_type=F32) + base
        place = jnp.sum(onehot * (count + names.astype(F32) * float(slots)), axis=0, keepdims=True)
        base = base + jnp.sum(onehot, axis=1, keepdims=True)
        lo = s % sides * rows_here
        code[s // sides, :, lo : lo + rows_here] = jnp.broadcast_to(place, (8, rows_here))

    for r in range(1, n):
        pre_copy(r).wait()
    for src in range(line):
        arrived(src * sides + 1 - b)

    standing = lax.broadcasted_iota(jnp.int32, (slots, block), 0).astype(F32)

    def landing(o, t):
        first = (o * slots).astype(F32)
        return (standing == code[t, 0:1, :] - first).astype(F32).astype(BF16)

    def tokens(t, carry):
        def gather(o, total):
            return total + jnp.dot(pre_got[o], landing(o, t), preferred_element_type=F32)

        pre = lax.fori_loop(0, n, gather, jnp.zeros((mine, block), F32))
        cdf = 0.5 * (1.0 + lax.erf(pre * 0.5**0.5))
        slope = cdf + pre * jnp.exp(-0.5 * pre * pre) * (2.0 * math.pi) ** (-0.5)
        rows = jnp.concatenate([mall[t * sides + i] for i in range(sides)], axis=0)
        linear = lax.dot_general(
            w_ref[...], rows, (((1,), (1,)), ((), ())), preferred_element_type=F32
        )
        act[t] = (pre * cdf).astype(BF16)
        hid[t] = (linear * slope).astype(BF16)
        return carry

    lax.fori_loop(0, blocks, tokens, 0)

    def outgoing(o, carry):
        def gather(t, total):
            return total + lax.dot_general(
                hid[t], landing(o, t), (((1,), (1,)), ((), ())), preferred_element_type=F32
            )

        hid_out[o] = lax.fori_loop(0, blocks, gather, jnp.zeros((mine, slots), F32)).astype(BF16)
        return carry

    lax.fori_loop(0, n, outgoing, 0)
    for r in range(1, n):
        hidden_copy(r).start()
    own = pltpu.make_async_copy(hid_out.at[me], h_out.at[me], local_sem.at[3])
    own.start()

    width = full.shape[1]

    def partial(t, carry):
        rows = jnp.concatenate([mall[t * sides + i] for i in range(sides)], axis=0)
        full[...] += jnp.dot(act[t], rows, preferred_element_type=F32)
        return carry

    full[...] = jnp.zeros_like(full)
    lax.fori_loop(0, blocks, partial, 0)
    piece = width // replicas
    for d in range(replicas):
        lo = d * piece // LANES * LANES
        hi = -(-(d + 1) * piece // LANES) * LANES
        shift = d * piece - lo
        value = full[:, lo:hi]
        if shift:
            value = pltpu.roll(value, hi - lo - shift, 1)
        part[d] = value[:, :piece]
    for r in range(1, replicas):
        part_copy(r).start()
    for r in range(1, replicas):
        part_copy(r).wait()
    total = part[rep]
    for r in range(1, replicas):
        total = total + part_got[r - 1]
    wg_out[...] = total

    own.wait()
    for r in range(1, n):
        hidden_copy(r).wait()

    def sent(t, carry):
        @pl.when((a - t >= 0) & (a + 1 < line))
        def _():
            up_copy(t, mall.at[me]).wait_send()

        @pl.when((a + t < line) & (a > 0))
        def _():
            down_copy(t, mall.at[me]).wait_send()

        side_copy(t, mall.at[me]).wait_send()
        return carry

    lax.fori_loop(0, line, sent, 0)


def fused(merged_grad, merged_owner, merger_pre, fc2_weight, query, key_states, value_states, out_grad, position):
    rows_here, width = merged_grad.shape
    n, replicas = lax.axis_size("ctx"), lax.axis_size("dp")
    slots, units = merger_pre.shape
    mine = units // n
    block, blocks = 2 * rows_here, n // 2
    piece = width // replicas
    cosine, sine = rope_tables(position)
    pre = jnp.transpose(merger_pre).reshape(n, mine, slots)
    owner = jnp.broadcast_to(merged_owner.reshape(1, rows_here), (8, rows_here))
    vmem = pl.BlockSpec(memory_space=pltpu.VMEM)
    dma = pltpu.SemaphoreType.DMA
    like = jax.ShapeDtypeStruct(query.shape, BF16)
    hidden, weight, *attention = pl.pallas_call(
        functools.partial(fused_kernel, n, replicas),
        in_specs=[vmem] * 10,
        out_specs=[vmem] * 5,
        out_shape=[
            jax.ShapeDtypeStruct((n, mine, slots), BF16),
            jax.ShapeDtypeStruct((mine, piece), F32),
            like,
            like,
            like,
        ],
        scratch_shapes=[
            pltpu.VMEM((n, rows_here, width), BF16),
            pltpu.VMEM((n, 8, rows_here), jnp.int32),
            pltpu.VMEM((n, mine, slots), BF16),
            pltpu.VMEM((blocks, 8, block), F32),
            pltpu.VMEM((blocks, mine, block), BF16),
            pltpu.VMEM((blocks, mine, block), BF16),
            pltpu.VMEM((n, mine, slots), BF16),
            pltpu.VMEM((mine, width), F32),
            pltpu.VMEM((replicas, mine, piece), F32),
            pltpu.VMEM((replicas - 1, mine, piece), F32),
            dma((n,)),
            dma((blocks,)),
            dma((blocks,)),
            dma((blocks,)),
            dma((n - 1,)),
            dma((n - 1,)),
            dma((n - 1,)),
            dma((n - 1,)),
            dma((n - 1,)),
            dma((n - 1,)),
            dma((replicas - 1,)),
            dma((replicas - 1,)),
            dma((4,)),
        ],
        compiler_params=pltpu.CompilerParams(
            collective_id=0, has_side_effects=True, vmem_limit_bytes=60 * 2**20
        ),
        name="fused",
    )(merged_grad, owner, pre, fc2_weight, query, key_states, value_states, out_grad, cosine, sine)
    hidden_grad = jnp.transpose(hidden.reshape(units, slots))
    weight_grad = weight * (rows_here * n * replicas) ** (-0.5)
    return (hidden_grad, weight_grad, *attention)


def solution(mesh):
    every = P(("dp", "ctx"), None)
    return jax.shard_map(
        fused,
        mesh=mesh,
        in_specs=(every, every, every, P("ctx", None)) + (every,) * 4 + (P(None, ("dp", "ctx")),),
        out_specs=(every, P("ctx", "dp")) + (every,) * 3,
        check_vma=False,
    )
```

profile of v0, /device:TPU:0, one launch (start us, length us, event | category | flops | bytes accessed | tf_op | source)
XLA Modules:
  0.0 141.6 jit_solution(4514977687650986254)
XLA Ops:
  0.6 0.0 copy-start
  0.7 0.1 pad.5.clone
  0.7 0.8 slice_convert_fusion.1
  1.5 1.2 broadcast_in_dim.7.o_ref
  2.8 0.1 broadcast_multiply_fusion.2
  2.8 0.2 fusion
  3.0 0.1 copy.23
  3.1 0.1 copy.21
  3.2 0.8 maximum_maximum_fusion.1
  4.1 0.0 copy-done
  4.1 1.4 %copy.20 = bf16[2560,256]{1,0:T(8,128)(2,1)} copy(bf16[2560,256]{0,1:T(8,128)(2,1)S(1)} %bitcast.8) | data formatting | bytes 2621440 | tf_op jit(solution)/shard_map/transpose | solution.py:392
  5.5 129.7 %fused.1 = (bf16[8,320,256]{2,1,0:T(8,128)(2,1)}, f32[320,448]{1,0:T(8,128)}, bf16[256,1280]{1,0:T(8,128)(2,1)}, bf16[256,1280]{1,0:T(8,128)(2,1)}, bf16[256,1280]{1,0:T(8,128)(2,1)}) custom-call(bf16[128,1792]{1,0:T(8,128)(2,1)} %m_ref.1, s32[8,128]{1,0:T(8,128)} %broadcast_in_dim.7.o_ref, bf16[8,320,256]{2,1,0:T(8,128)(2,1)} %bitcast.7, ...), custom_call_target="tpu_custom_call" | custom-call | tf_op jit(solution)/shard_map/fused/pallas_call | solution.py:397
  135.2 0.0 copy-start.4
  135.2 2.5 %copy.25 = bf16[2560,256]{0,1:T(8,128)(2,1)} copy(bf16[2560,256]{1,0:T(8,128)(2,1)} %bitcast.10) | data formatting | bytes 2621440 | tf_op jit(solution)/shard_map/reshape | solution.py:438
  137.7 0.0 copy-start.3
  137.7 0.0 copy-done.4
  137.7 0.0 copy-start.2
  137.7 0.9 broadcast_multiply_fusion
  138.6 0.4 copy-done.3
  139.1 0.0 copy-start.1
  139.1 0.8 copy.29
  139.9 0.0 copy-done.2
  139.9 0.8 copy.30
  140.7 0.0 copy-done.1
  140.7 0.8 copy.31
  (3 shorter events, 0.0 us)
Async XLA Ops:
  0.6 3.4 %copy-start = (bf16[256,2560]{1,0:T(8,128)(2,1)S(1)}, bf16[256,2560]{1,0:T(8,128)(2,1)}, u32[]{:S(2)}) copy-start(bf16[256,2560]{1,0:T(8,128)(2,1)} %param.11) | copy-start | bytes 3932164
  135.2 2.5 %copy-start.4 = (f32[320,448]{1,0:T(8,128)S(1)}, f32[320,448]{1,0:T(8,128)}, u32[]{:S(2)}) copy-start(f32[320,448]{1,0:T(8,128)} %get-tuple-element.11) | copy-start | bytes 1720324
  137.7 1.3 copy-start.3
  137.7 2.2 %copy-start.2 = (bf16[256,1280]{1,0:T(8,128)(2,1)S(1)}, bf16[256,1280]{1,0:T(8,128)(2,1)}, u32[]{:S(2)}) copy-start(bf16[256,1280]{1,0:T(8,128)(2,1)} %get-tuple-element.31) | copy-start | bytes 1966084
  139.1 1.7 %copy-start.1 = (bf16[256,1280]{1,0:T(8,128)(2,1)S(1)}, bf16[256,1280]{1,0:T(8,128)(2,1)}, u32[]{:S(2)}) copy-start(bf16[256,1280]{1,0:T(8,128)(2,1)} %get-tuple-element.32) | copy-start | bytes 1966084
where the time goes:
time: 142 us
  Pallas kernels  130 us (92%)
  local copies, waits for them, and re-layouts  8.38 us (6%)
  other arithmetic  2.78 us (2%)
    pallas_call x1, Pallas kernels, fused(): pl.pallas_call(functools.partial(fused_kernel, n, replicas), in_specs=[vm...  130 us
    unnamed x13, local copies, waits for them, and re-layouts  2.95 us

commit v1 on v0

v1 whole, which is shorter than its diff:
```python
import functools
import math

import jax
import jax.numpy as jnp
from jax import lax
from jax.experimental import pallas as pl
from jax.experimental.pallas import tpu as pltpu
from jax.sharding import PartitionSpec as P

HEAD = 80
WIN = 64
LANES = 128
SIDES = 2
F32 = jnp.float32
BF16 = jnp.bfloat16
MESH = pl.DeviceIdType.MESH
NT = (((1,), (1,)), ((), ()))
TN = (((0,), (0,)), ((), ()))
NN = (((1,), (0,)), ((), ()))


def dot(a, b, dims=NN):
    return lax.dot_general(a, b, dims, preferred_element_type=F32)


def spread(table, width):
    shape = (LANES, width)
    lane = lax.broadcasted_iota(jnp.int32, shape, 1) % HEAD
    pick = (lane == lax.broadcasted_iota(jnp.int32, shape, 0)).astype(F32).astype(BF16)
    high = table.astype(BF16)
    rest = table - high.astype(F32)
    mid = rest.astype(BF16)
    low = (rest - mid.astype(F32)).astype(BF16)
    return dot(high, pick) + dot(mid, pick) + dot(low, pick)


def rope_tables(pos_ref, freq_ref, c_ref, s_ref):
    count = pos_ref.shape[1]
    half, quarter = HEAD // 2, HEAD // 4
    unit = lax.broadcasted_iota(jnp.int32, (LANES, count), 0)
    rows = pos_ref[0:1, :].astype(F32)
    cols = pos_ref[1:2, :].astype(F32)
    freq = jnp.transpose(jnp.broadcast_to(freq_ref[...], (count, LANES)))
    angles = jnp.where(unit % half < quarter, rows, cols) * freq
    c_ref[...] = jnp.transpose(jnp.cos(angles))
    s_ref[...] = jnp.transpose(jnp.where(unit < half, -1.0, 1.0) * jnp.sin(angles))


def attention_part(at, over, refs, c_ref, s_ref, outs):
    q_ref, k_ref, v_ref, g_ref = refs
    dq_ref, dk_ref, dv_ref = outs
    width = over.size
    heads = width // HEAD
    half = HEAD // 2
    cosine = spread(c_ref[at, :], width)
    sine = spread(s_ref[at, :], width)
    lane = lax.broadcasted_iota(jnp.int32, (WIN, width), 1)
    first = lane % HEAD < half

    def swap(x):
        return jnp.where(first, pltpu.roll(x, width - half, 1), pltpu.roll(x, half, 1))

    def rotated(x):
        return (x * cosine + swap(x) * sine).astype(BF16)

    def unrotated(x):
        return (x * cosine - swap(x) * sine).astype(BF16)

    q = rotated(q_ref[at, over].astype(F32))
    k = rotated(k_ref[at, over].astype(F32))
    v = v_ref[at, over]
    g = g_ref[at, over]
    factor = HEAD ** (-0.5)
    dq, dk, dv = {}, {}, {}

    def add(into, tile, value):
        for i in range(value.shape[1] // LANES):
            part = value[:, i * LANES : (i + 1) * LANES]
            into[tile + i] = into[tile + i] + part if tile + i in into else part

    for head in range(heads):
        tile = head * HEAD // LANES
        end = -(-(head + 1) * HEAD // LANES)
        lo, hi = tile * LANES, end * LANES
        here = lax.broadcasted_iota(jnp.int32, (1, hi - lo), 1) + lo
        mask = ((here >= head * HEAD) & (here < (head + 1) * HEAD)).astype(F32).astype(BF16)
        qm = q[:, lo:hi] * mask
        km = k[:, lo:hi] * mask
        gm = g[:, lo:hi] * mask
        scores = dot(qm, k[:, lo:hi], NT) * factor
        weight = jnp.exp(scores - jnp.max(scores, axis=1, keepdims=True))
        probs = weight * (1.0 / jnp.sum(weight, axis=1, keepdims=True))
        probs_b = probs.astype(BF16)
        prob_grad = dot(gm, v[:, lo:hi], NT)
        delta = jnp.sum(probs_b.astype(F32) * prob_grad, axis=1, keepdims=True)
        score_grad = (probs * (prob_grad - delta)).astype(BF16)
        add(dv, tile, dot(probs_b, gm, TN))
        add(dq, tile, dot(score_grad, km, NN))
        add(dk, tile, dot(score_grad, qm, TN))

    def joined(parts):
        return jnp.concatenate([parts[i] for i in range(width // LANES)], axis=1)

    dq_ref[at, over] = unrotated(joined(dq) * factor)
    dk_ref[at, over] = unrotated(joined(dk) * factor)
    dv_ref[at, over] = joined(dv).astype(BF16)


def fused_kernel(
    n,
    replicas,
    m_hbm,
    o_ref,
    p_hbm,
    w_hbm,
    q_hbm,
    k_hbm,
    v_hbm,
    g_hbm,
    pos_ref,
    freq_ref,
    h_hbm,
    wg_hbm,
    dq_hbm,
    dk_hbm,
    dv_hbm,
    mall,
    owners,
    pre,
    slope,
    pre_send,
    pre_got,
    fall,
    w_ref,
    code,
    slotted,
    hid,
    hid_out,
    hid_got,
    h_ref,
    full,
    part,
    core_got,
    x_got,
    wg_ref,
    q_ref,
    k_ref,
    v_ref,
    g_ref,
    dq_ref,
    dk_ref,
    dv_ref,
    c_ref,
    s_ref,
    m_recv,
    up_sem,
    down_sem,
    side_sem,
    o_send,
    o_recv,
    p_send,
    p_recv,
    f_recv,
    mirror_sem,
    fup_sem,
    fdown_sem,
    fside_sem,
    fx_sem,
    fcore_sem,
    h_send,
    h_recv,
    c_send,
    c_recv,
    x_send,
    x_recv,
    local_sem,
    out_sem,
):
    line = n // SIDES
    near = n // 2
    near_line = line // 2
    rows_here, width = m_hbm.shape
    slots, units = pre.shape
    mine = units // n
    parts = w_hbm.shape[0]
    shared = parts > 1
    block = SIDES * rows_here
    patches, features = q_ref.shape
    chips = replicas // 2
    me = lax.axis_index("ctx")
    rep = lax.axis_index("dp")
    a, b = me // SIDES, me % SIDES
    side, row = a // near_line, a % near_line
    here = me % near
    mirror = (me + near) % n
    partner = rep // 2 * 2 + 1 - rep % 2
    core = rep % 2
    q_own = rep if shared else 0
    q_far = (rep + 2) % replicas if shared else 0

    barrier = pltpu.get_barrier_semaphore()
    for r in range(1, n):
        pl.semaphore_signal(barrier, inc=1, device_id={"dp": rep, "ctx": (me + r) % n}, device_id_type=MESH)
    pl.semaphore_signal(barrier, inc=1, device_id={"dp": partner, "ctx": me}, device_id_type=MESH)
    for r in range(1, chips):
        pl.semaphore_signal(
            barrier, inc=1, device_id={"dp": (rep + 2 * r) % replicas, "ctx": me}, device_id_type=MESH
        )
    locals_ = [
        pltpu.make_async_copy(p_hbm, pre, local_sem.at[0]),
        pltpu.make_async_copy(q_hbm, q_ref, local_sem.at[1]),
        pltpu.make_async_copy(k_hbm, k_ref, local_sem.at[2]),
        pltpu.make_async_copy(v_hbm, v_ref, local_sem.at[3]),
        pltpu.make_async_copy(g_hbm, g_ref, local_sem.at[4]),
        pltpu.make_async_copy(m_hbm, mall.at[me], local_sem.at[5]),
        pltpu.make_async_copy(w_hbm, w_ref, local_sem.at[6]),
        pltpu.make_async_copy(o_ref, owners.at[me], local_sem.at[7]),
    ]
    for copy in locals_:
        copy.start()
    pl.semaphore_wait(barrier, n - 1 + chips)

    def send(src, dst, send_sem, recv_sem, ctx=None, dp=None):
        where = {"dp": rep if dp is None else dp, "ctx": me if ctx is None else ctx}
        return pltpu.make_async_remote_copy(
            src_ref=src,
            dst_ref=dst,
            send_sem=send_sem,
            recv_sem=recv_sem,
            device_id=where,
            device_id_type=MESH,
        )

    def owner_copy(r):
        return send(o_ref, owners.at[me], o_send.at[r - 1], o_recv.at[r - 1], ctx=(me + r) % n)

    def unit_rows(peer):
        return pre_send.at[pl.ds(pl.multiple_of(peer * mine, 16), mine), :]

    def pre_copy(r):
        peer = (me + r) % n
        return send(unit_rows(peer), pre_got.at[me], p_send.at[r - 1], p_recv.at[r - 1], ctx=peer)

    def hidden_copy(r):
        to = (here + r) % near
        return send(
            hid_out.at[to], hid_got.at[here], h_send.at[r - 1], h_recv.at[r - 1], ctx=side * near + to
        )

    def up_copy(t, ref):
        at = (a - t) * SIDES + b
        return send(ref, mall.at[at], up_sem.at[t], m_recv.at[at], ctx=me + SIDES)

    def down_copy(t, ref):
        at = (a + t) * SIDES + b
        return send(ref, mall.at[at], down_sem.at[t], m_recv.at[at], ctx=me - SIDES)

    def side_copy(at, ref):
        src = at * SIDES + b
        return send(ref, mall.at[src], side_sem.at[at], m_recv.at[src], ctx=a * SIDES + 1 - b)

    def m_arrived(src):
        send(mall.at[src], mall.at[src], up_sem.at[0], m_recv.at[src], ctx=a * SIDES + 1 - b).wait_recv()

    def mirror_copy():
        return send(
            w_hbm.at[q_own], fall.at[here, q_own], mirror_sem.at[0], f_recv.at[here, q_own], ctx=mirror
        )

    def fup_copy(t):
        at = (row - t) * SIDES + b
        ref = fall.at[at, q_own]
        return send(ref, ref, fup_sem.at[t], f_recv.at[at, q_own], ctx=me + SIDES)

    def fdown_copy(t):
        at = (row + t) * SIDES + b
        ref = fall.at[at, q_own]
        return send(ref, ref, fdown_sem.at[t], f_recv.at[at, q_own], ctx=me - SIDES)

    def fside_copy(at):
        src = at * SIDES + b
        ref = fall.at[src, q_own]
        return send(ref, ref, fside_sem.at[at], f_recv.at[src, q_own], ctx=a * SIDES + 1 - b)

    def fx_copy(src):
        ref = fall.at[src, q_own]
        return send(ref, ref, fx_sem.at[src], f_recv.at[src, q_own], dp=q_far)

    def fcore_copy(src, which):
        at = (q_own, q_far)[which]
        ref = fall.at[src, at]
        return send(ref, ref, fcore_sem.at[src, which], f_recv.at[src, at], dp=partner)

    def f_arrived(src, at):
        ref = fall.at[src, at]
        send(ref, ref, fup_sem.at[0], f_recv.at[src, at], ctx=a * SIDES + 1 - b).wait_recv()

    def core_copy(x):
        return send(
            part.at[2 * x + 1 - core], core_got.at[x], c_send.at[x], c_recv.at[x], dp=partner
        )

    def x_copy(r):
        peer = (rep + 2 * r) % replicas
        return send(part.at[peer], x_got.at[r - 1], x_send.at[r - 1], x_recv.at[r - 1], dp=peer)

    def when(condition, body):
        pl.when(condition)(body)

    for r in range(1, n):
        owner_copy(r).start()
    when(a + 1 < line, lambda: up_copy(0, m_hbm).start())
    when(a > 0, lambda: down_copy(0, m_hbm).start())
    side_copy(a, m_hbm).start()
    mirror_copy().start()

    locals_[0].wait()

    def turn(j, carry):
        over = pl.ds(pl.multiple_of(j * LANES, LANES), LANES)
        pre_send[over, :] = jnp.transpose(pre[:, over].astype(F32)).astype(BF16)
        return carry

    lax.fori_loop(0, units // LANES, turn, 0)
    own_pre = pltpu.make_async_copy(unit_rows(me), pre_got.at[me], local_sem.at[8])
    own_pre.start()
    rope_tables(pos_ref, freq_ref, c_ref, s_ref)
    full[...] = jnp.zeros_like(full)
    slotted[...] = jnp.zeros_like(slotted)
    for copy in locals_[1:5]:
        copy.wait()

    def both(t, at, count, body):
        if t == 0:
            body(at, None)
        else:
            when(at - t >= 0, lambda: body(at - t, True))
            when(at + t < count, lambda: body(at + t, False))

    def send_pre():
        for r in range(1, n):
            pre_copy(r).start()

    def token_event(t):
        def body(at, below):
            src = at * SIDES + b
            ref = mall.at[src]
            m_arrived(src)
            if below:
                when(a + 1 < line, lambda: up_copy(t, ref).start())
            else:
                when(a > 0, lambda: down_copy(t, ref).start())
            side_copy(at, ref).start()

        both(t, a, line, body)

    def across(src):
        if shared:
            fx_copy(src).start()
            fcore_copy(src, 0).start()

    def weight_event(t):
        def body(at, below):
            src = at * SIDES + b
            f_arrived(src, q_own)
            if below is not False:
                when(row + 1 < near_line, lambda: fup_copy(t).start())
            if below is not True:
                when(row > 0, lambda: fdown_copy(t).start())
            fside_copy(at).start()
            across(src)

        both(t, row, near_line, body)

    def weight_side_event(t):
        def body(at, below):
            src = at * SIDES + 1 - b
            f_arrived(src, q_own)
            across(src)

        both(t, row, near_line, body)

    def weight_far_event(t, other):
        def body(at, below):
            src = at * SIDES + (1 - b if other else b)
            if shared:
                f_arrived(src, q_far)
                fcore_copy(src, 1).start()

        both(t, row, near_line, body)

    def event(kind, *given):
        return functools.partial(kind, *given)

    order = [(1, event(token_event, 1))]
    if line > 2:
        order += [(3, event(token_event, 2))]
    order += [(3, send_pre)]
    for t in range(near_line):
        order += [(4 + 2 * t, event(weight_event, t)), (4 + 2 * t, event(weight_side_event, t))]
    for t in range(3, line):
        order += [(8, event(token_event, t))]
    for t in range(near_line):
        order += [(6 + 2 * t, event(weight_far_event, t, False)), (6 + 2 * t, event(weight_far_event, t, True))]

    halves = 2
    span = features // halves
    steps = patches // WIN * halves

    def attend(i, carry):
        at = pl.ds(pl.multiple_of(i // halves * WIN, WIN), WIN)
        over = pl.ds(pl.multiple_of(i % halves * span, LANES), span)
        attention_part(
            at, over, (q_ref, k_ref, v_ref, g_ref), c_ref, s_ref, (dq_ref, dk_ref, dv_ref)
        )
        for step in range(steps):
            todo = [run for index, run in order if index == step]
            if todo:
                when(i == step, lambda todo=todo: [run() for run in todo] and None)
        return carry

    lax.fori_loop(0, steps, attend, 0)
    outs = [
        pltpu.make_async_copy(dq_ref, dq_hbm, out_sem.at[0]),
        pltpu.make_async_copy(dk_ref, dk_hbm, out_sem.at[1]),
        pltpu.make_async_copy(dv_ref, dv_hbm, out_sem.at[2]),
    ]
    for copy in outs:
        copy.start()

    far = (1 - side) * (units // 2)

    def incline(j, carry):
        x = pre[:, pl.ds(pl.multiple_of(far + j * LANES, LANES), LANES)].astype(F32)
        cdf = 0.5 * (1.0 + lax.erf(x * 0.5**0.5))
        slope[:, pl.ds(pl.multiple_of(j * LANES, LANES), LANES)] = cdf + x * jnp.exp(-0.5 * x * x) * (
            2.0 * math.pi
        ) ** (-0.5)
        return carry

    lax.fori_loop(0, units // 2 // LANES, incline, 0)

    for copy in locals_[5:]:
        copy.wait()
    for r in range(1, n):
        owner_copy(r).wait()
    padded = -(-n // 16) * 16
    earlier = lax.broadcasted_iota(jnp.int32, (rows_here, rows_here), 0) < lax.broadcasted_iota(
        jnp.int32, (rows_here, rows_here), 1
    )
    earlier = earlier.astype(F32).astype(BF16)
    names = lax.broadcasted_iota(jnp.int32, (padded, rows_here), 0)
    base = jnp.zeros((padded, 1), F32)
    for s in range(n):
        onehot = (names == owners[s]).astype(F32)
        count = dot(onehot.astype(BF16), earlier) + base
        position = jnp.sum(onehot * (count + names.astype(F32) * float(slots)), axis=0, keepdims=True)
        base = base + jnp.sum(onehot, axis=1, keepdims=True)
        lo = s % SIDES * rows_here
        code[s // SIDES, :, lo : lo + rows_here] = jnp.broadcast_to(position, (8, rows_here))
    standing = lax.broadcasted_iota(jnp.int32, (slots, block), 0).astype(F32)

    def landing(o, t):
        first = (o * slots).astype(F32)
        return (standing == code[t, 0:1, :] - first).astype(F32).astype(BF16)

    for index, run in sorted((pair for pair in order if pair[0] >= steps), key=lambda pair: pair[0]):
        run()
    for r in range(1, n):
        pre_copy(r).wait()
    own_pre.wait()

    def tokens(d, carry):
        low = jnp.where(d <= a, a - d, d)
        flip = line - 1 - a
        high = line - 1 - jnp.where(d <= flip, flip - d, d)
        t = jnp.where(side == 0, low, high)
        m_arrived(t * SIDES + 1 - b)

        def gather(o, total):
            return total + dot(pre_got[o], landing(o, t))

        x = lax.fori_loop(0, n, gather, jnp.zeros((mine, block), F32))
        cdf = 0.5 * (1.0 + lax.erf(x * 0.5**0.5))
        incline = cdf + x * jnp.exp(-0.5 * x * x) * (2.0 * math.pi) ** (-0.5)
        rows = jnp.concatenate([mall[t * SIDES + i] for i in range(SIDES)], axis=0)
        hid[t] = (dot(w_ref[...].reshape(mine, width), rows, NT) * incline).astype(BF16)
        full[...] += dot((x * cdf).astype(BF16), rows)
        slotted[...] += dot(landing(me, t), rows).astype(BF16)
        return carry

    lax.fori_loop(0, line, tokens, 0)

    piece = width // replicas
    for d in range(replicas):
        lo = d * piece // LANES * LANES
        hi = -(-(d + 1) * piece // LANES) * LANES
        shift = d * piece - lo
        value = full[:, lo:hi]
        if shift:
            value = pltpu.roll(value, hi - lo - shift, 1)
        part[d] = value[:, :piece]
    for x in range(chips):
        core_copy(x).start()

    def outgoing(i, carry):
        def gather(t, total):
            return total + dot(hid[t], landing(side * near + i, t), NT)

        hid_out[i] = lax.fori_loop(0, line, gather, jnp.zeros((mine, slots), F32)).astype(BF16)
        return carry

    lax.fori_loop(0, near, outgoing, 0)
    for r in range(1, near):
        hidden_copy(r).start()
    own_hidden = pltpu.make_async_copy(hid_out.at[here], hid_got.at[here], local_sem.at[9])
    own_hidden.start()

    for x in range(chips):
        core_copy(x).wait()
    for x in range(chips):
        part[2 * x + core] = part[2 * x + core] + core_got[x]
    for r in range(1, chips):
        x_copy(r).start()

    groups = next(g for g in range(near_line, 0, -1) if near_line % g == 0 and units // 2 // g % LANES == 0)
    run, each = near // groups, units // 2 // groups

    def h_copy(g, start):
        over = pl.ds(pl.multiple_of(start + g * each, LANES), each)
        return pltpu.make_async_copy(h_ref.at[:, over], h_hbm.at[:, over], out_sem.at[3])

    def linear(g, carry):
        if shared:

            def await_rest(i, carry):
                for other in (partner, (partner + 2) % replicas):
                    f_arrived(g * run + i, other)
                return carry

            lax.fori_loop(0, run, await_rest, 0)
        weight = fall[pl.ds(g * run, run)].reshape(each, width)
        over = pl.ds(pl.multiple_of(g * each, LANES), each)
        to = pl.ds(pl.multiple_of(far + g * each, LANES), each)
        h_ref[:, to] = (dot(slotted[...], weight, NT) * slope[:, over]).astype(BF16)
        return carry

    lax.fori_loop(0, groups, linear, 0)

    own_hidden.wait()
    for r in range(1, near):
        hidden_copy(r).wait()
    spot = lax.broadcasted_iota(jnp.int32, (slots, slots), 0) == lax.broadcasted_iota(
        jnp.int32, (slots, slots), 1
    )
    spot = spot.astype(F32).astype(BF16)

    def settle(g, carry):
        rows = hid_got[pl.ds(g * run, run)].reshape(each, slots)
        to = pl.ds(pl.multiple_of(side * (units // 2) + g * each, LANES), each)
        h_ref[:, to] = dot(spot, rows, NT).astype(BF16)
        return carry

    lax.fori_loop(0, groups, settle, 0)
    outs.append(pltpu.make_async_copy(h_ref, h_hbm, out_sem.at[3]))
    outs[-1].start()

    total = part[rep]
    for r in range(1, chips):
        x_copy(r).wait()
        total = total + x_got[r - 1]
    wg_ref[...] = total * (rows_here * n * replicas) ** (-0.5)
    outs.append(pltpu.make_async_copy(wg_ref, wg_hbm, out_sem.at[4]))
    outs[-1].start()

    def sent(t, carry):
        @pl.when((a - t >= 0) & (a + 1 < line))
        def _():
            up_copy(t, mall.at[me]).wait_send()

        @pl.when((a + t < line) & (a > 0))
        def _():
            down_copy(t, mall.at[me]).wait_send()

        side_copy(t, mall.at[me]).wait_send()
        return carry

    lax.fori_loop(0, line, sent, 0)
    mirror_copy().wait_send()

    def weight_sent(t, carry):
        @pl.when((row - t >= 0) & (row + 1 < near_line))
        def _():
            fup_copy(t).wait_send()

        @pl.when((row + t < near_line) & (row > 0))
        def _():
            fdown_copy(t).wait_send()

        fside_copy(t).wait_send()
        return carry

    lax.fori_loop(0, near_line, weight_sent, 0)
    if shared:

        def passed(src, carry):
            fx_copy(src).wait_send()
            fcore_copy(src, 0).wait_send()
            fcore_copy(src, 1).wait_send()
            return carry

        lax.fori_loop(0, near, passed, 0)
    for copy in outs:
        copy.wait()


def finish_kernel(*refs):
    ins, outs, held = refs[:5], refs[5:10], refs[10:15]
    in_sem, out_sem = refs[15:]
    first = [pltpu.make_async_copy(ins[i], held[i], in_sem.at[i]) for i in range(5)]
    second = [pltpu.make_async_copy(held[i], outs[i], out_sem.at[i]) for i in range(5)]
    for copy in first:
        copy.start()
    for i in range(5):
        first[i].wait()
        second[i].start()
    for copy in second:
        copy.wait()


def fused(merged_grad, merged_owner, merger_pre, fc2_weight, query, key_states, value_states, out_grad, position):
    rows_here, width = merged_grad.shape
    n, replicas = lax.axis_size("ctx"), lax.axis_size("dp")
    slots, units = merger_pre.shape
    mine = units // n
    line = n // SIDES
    near = n // 2
    near_line = line // 2
    block = SIDES * rows_here
    piece = width // replicas
    chips = replicas // 2
    parts = replicas if chips == 2 and mine % (16 * replicas) == 0 else 1
    quarter = HEAD // 4
    freq = 1.0 / 10000.0 ** (jnp.arange(quarter, dtype=F32) * (4.0 / HEAD))
    freq = jnp.concatenate([freq] * 4 + [jnp.zeros((LANES - HEAD,), F32)]).reshape(1, LANES)
    vmem = pl.BlockSpec(memory_space=pltpu.VMEM)
    hbm = pl.BlockSpec(memory_space=pl.ANY)
    dma = pltpu.SemaphoreType.DMA
    like = jax.ShapeDtypeStruct(query.shape, BF16)
    shapes = [
        jax.ShapeDtypeStruct((slots, units), BF16),
        jax.ShapeDtypeStruct((mine, piece), F32),
        like,
        like,
        like,
    ]
    results = pl.pallas_call(
        functools.partial(fused_kernel, n, replicas),
        in_specs=[hbm, vmem] + [hbm] * 6 + [vmem] * 2,
        out_specs=[hbm] * 5,
        out_shape=shapes,
        scratch_shapes=[
            pltpu.VMEM((n, rows_here, width), BF16),
            pltpu.VMEM((n, 1, rows_here), jnp.int32),
            pltpu.VMEM((slots, units), BF16),
            pltpu.VMEM((slots, units // 2), F32),
            pltpu.VMEM((units, slots), BF16),
            pltpu.VMEM((n, mine, slots), BF16),
            pltpu.VMEM((near, parts, mine // parts, width), BF16),
            pltpu.VMEM((parts, mine // parts, width), BF16),
            pltpu.VMEM((line, 8, block), F32),
            pltpu.VMEM((slots, width), BF16),
            pltpu.VMEM((line, mine, block), BF16),
            pltpu.VMEM((near, mine, slots), BF16),
            pltpu.VMEM((near, mine, slots), BF16),
            pltpu.VMEM((slots, units), BF16),
            pltpu.VMEM((mine, width), F32),
            pltpu.VMEM((replicas, mine, piece), F32),
            pltpu.VMEM((chips, mine, piece), F32),
            pltpu.VMEM((max(chips - 1, 1), mine, piece), F32),
            pltpu.VMEM((mine, piece), F32),
        ]
        + [pltpu.VMEM(query.shape, BF16)] * 7
        + [
            pltpu.VMEM((query.shape[0], LANES), F32),
            pltpu.VMEM((query.shape[0], LANES), F32),
            dma((n,)),
            dma((line,)),
            dma((line,)),
            dma((line,)),
            dma((n - 1,)),
            dma((n - 1,)),
            dma((n - 1,)),
            dma((n - 1,)),
            dma((near, parts)),
            dma((1,)),
            dma((near_line,)),
            dma((near_line,)),
            dma((near_line,)),
            dma((near,)),
            dma((near, 2)),
            dma((near - 1,)),
            dma((near - 1,)),
            dma((chips,)),
            dma((chips,)),
            dma((max(chips - 1, 1),)),
            dma((max(chips - 1, 1),)),
            dma((10,)),
            dma((5,)),
        ],
        compiler_params=pltpu.CompilerParams(
            collective_id=0, has_side_effects=True, vmem_limit_bytes=60 * 2**20
        ),
        name="fused",
    )(
        merged_grad,
        merged_owner.reshape(1, rows_here),
        merger_pre,
        fc2_weight.reshape(parts, mine // parts, width),
        query,
        key_states,
        value_states,
        out_grad,
        position,
        freq,
    )
    return tuple(
        pl.pallas_call(
            finish_kernel,
            in_specs=[hbm] * 5,
            out_specs=[hbm] * 5,
            out_shape=shapes,
            scratch_shapes=[pltpu.VMEM(shape.shape, shape.dtype) for shape in shapes] + [dma((5,)), dma((5,))],
            name="finish",
        )(*results)
    )


def solution(mesh):
    every = P(("dp", "ctx"), None)
    return jax.shard_map(
        fused,
        mesh=mesh,
        in_specs=(every, every, every, P("ctx", None)) + (every,) * 4 + (P(None, ("dp", "ctx")),),
        out_specs=(every, P("ctx", "dp")) + (every,) * 3,
        check_vma=False,
    )
```

time: 142 us -> 136 us (0.958)
  local copies, waits for them, and re-layouts: 8.38 us -> 0.6 us
  Pallas kernels: 130 us -> 134 us
  other arithmetic: 2.78 us -> 0.01 us
    pallas_call x1 -> x2, Pallas kernels: 130 us -> 134 us  [the longest x1 131 us: fused(): pl.pallas_call(functools.partial(fused_kernel, n, replicas), in_specs=[hb...]
    unnamed x13 -> x0, local copies, waits for them, and re-layouts: 2.95 us -> none
    reshape x1 -> x0, local copies, waits for them, and re-layouts: 2.49 us -> none  [fused(): hidden_grad = jnp.transpose(hidden.reshape(units, slots))]
    transpose x1 -> x0, local copies, waits for them, and re-layouts: 1.43 us -> none  [fused(): pre = jnp.transpose(merger_pre).reshape(n, mine, slots)]
where the time goes in v1:
time: 136 us
  Pallas kernels  134 us (99%)
    pallas_call x1, Pallas kernels, fused(): pl.pallas_call(functools.partial(fused_kernel, n, replicas), in_specs=[hb...  131 us
    pallas_call x1, Pallas kernels, fused(): pl.pallas_call(finish_kernel, in_specs=[hbm] * 5, out_specs=[hbm] * 5, ou...  3.32 us

profile of v1, /device:TPU:0, one launch (start us, length us, event | category | flops | bytes accessed | tf_op | source)
XLA Modules:
  0.0 135.7 jit_solution(13290935979786284328)
XLA Ops:
  0.7 0.6 concatenate.3
  1.3 131.1 %fused.1 = (bf16[256,2560]{1,0:T(8,128)(2,1)}, f32[320,448]{1,0:T(8,128)}, bf16[256,1280]{1,0:T(8,128)(2,1)}, bf16[256,1280]{1,0:T(8,128)(2,1)}, bf16[256,1280]{1,0:T(8,128)(2,1)}) custom-call(bf16[128,1792]{1,0:T(8,128)(2,1)} %m_hbm.1, s32[1,128]{1,0:T(1,128)} %bitcast.5, bf16[256,2560]{1,0:T(8,128)(2,1)} %p_hbm.1, bf16[4,80,1792]{2,1,0:T(8,128)(2,1)} %bitcast.3, ...), custom_call_target="tpu_custom_call" | custom-call | tf_op jit(solution)/shard_map/fused/pallas_call | solution.py:658
  132.4 3.3 %finish.1 = (bf16[256,2560]{1,0:T(8,128)(2,1)}, f32[320,448]{1,0:T(8,128)}, bf16[256,1280]{1,0:T(8,128)(2,1)}, bf16[256,1280]{1,0:T(8,128)(2,1)}, bf16[256,1280]{1,0:T(8,128)(2,1)}) custom-call(bf16[256,2560]{1,0:T(8,128)(2,1)} %get-tuple-element.10.refs_0_, f32[320,448]{1,0:T(8,128)} %get-tuple-element.11.refs_1_, ...), custom_call_target="tpu_custom_call" | custom-call | tf_op jit(solution)/shard_map/finish/pallas_call | solution.py:729
  (2 shorter events, 0.0 us)

commit v2 on v1

--- a/solution.py
+++ b/solution.py
@@ -136,6 +136,7 @@
     code,
     slotted,
     hid,
+    linear_ref,
     hid_out,
     hid_got,
     h_ref,
@@ -238,9 +239,12 @@
     def unit_rows(peer):
         return pre_send.at[pl.ds(pl.multiple_of(peer * mine, 16), mine), :]
 
+    def pre_place():
+        return pre_got.at[:, pl.ds(pl.multiple_of(me * slots, LANES), slots)]
+
     def pre_copy(r):
         peer = (me + r) % n
-        return send(unit_rows(peer), pre_got.at[me], p_send.at[r - 1], p_recv.at[r - 1], ctx=peer)
+        return send(unit_rows(peer), pre_place(), p_send.at[r - 1], p_recv.at[r - 1], ctx=peer)
 
     def hidden_copy(r):
         to = (here + r) % near
@@ -323,7 +327,7 @@
         return carry
 
     lax.fori_loop(0, units // LANES, turn, 0)
-    own_pre = pltpu.make_async_copy(unit_rows(me), pre_got.at[me], local_sem.at[8])
+    own_pre = pltpu.make_async_copy(unit_rows(me), pre_place(), local_sem.at[8])
     own_pre.start()
     rope_tables(pos_ref, freq_ref, c_ref, s_ref)
     full[...] = jnp.zeros_like(full)
@@ -368,10 +372,12 @@
                 when(row + 1 < near_line, lambda: fup_copy(t).start())
             if below is not True:
                 when(row > 0, lambda: fdown_copy(t).start())
-            fside_copy(at).start()
             across(src)
 
         both(t, row, near_line, body)
+
+    def weight_turn(t):
+        both(t, row, near_line, lambda at, below: fside_copy(at).start())
 
     def weight_side_event(t):
         def body(at, below):
@@ -393,16 +399,17 @@
     def event(kind, *given):
         return functools.partial(kind, *given)
 
-    order = [(1, event(token_event, 1))]
-    if line > 2:
-        order += [(3, event(token_event, 2))]
-    order += [(3, send_pre)]
-    for t in range(near_line):
-        order += [(4 + 2 * t, event(weight_event, t)), (4 + 2 * t, event(weight_side_event, t))]
-    for t in range(3, line):
-        order += [(8, event(token_event, t))]
-    for t in range(near_line):
-        order += [(6 + 2 * t, event(weight_far_event, t, False)), (6 + 2 * t, event(weight_far_event, t, True))]
+    order = [
+        (1, event(token_event, 1)),
+        (2, event(weight_event, 0)),
+        (2, event(weight_turn, 0)),
+        (4, event(token_event, 2)),
+        (4, send_pre),
+        (5, event(weight_side_event, 0)),
+        (6, event(weight_event, 1)),
+        (6, event(weight_turn, 1)),
+        (6, event(weight_far_event, 0, False)),
+    ]
 
     halves = 2
     span = features // halves
@@ -465,32 +472,53 @@
         first = (o * slots).astype(F32)
         return (standing == code[t, 0:1, :] - first).astype(F32).astype(BF16)
 
-    for index, run in sorted((pair for pair in order if pair[0] >= steps), key=lambda pair: pair[0]):
-        run()
+    def nth(d):
+        low = jnp.where(d <= a, a - d, d)
+        flip = line - 1 - a
+        high = line - 1 - jnp.where(d <= flip, flip - d, d)
+        return jnp.where(side == 0, low, high)
+
+    def gathered(t):
+        return jnp.concatenate([mall[t * SIDES + i] for i in range(SIDES)], axis=0)
+
+    def early(d, carry):
+        t = nth(d)
+        m_arrived(t * SIDES + 1 - b)
+        rows = gathered(t)
+        linear_ref[t] = dot(w_ref[...].reshape(mine, width), rows, NT)
+        slotted[...] += dot(landing(me, t), rows).astype(BF16)
+        return carry
+
+
+    def late(d, carry):
+        t = nth(d)
+
+        spots = jnp.concatenate([landing(jnp.int32(o), t) for o in range(n)], axis=0)
+        x = dot(pre_got[...], spots)
+        cdf = 0.5 * (1.0 + lax.erf(x * 0.5**0.5))
+        incline = cdf + x * jnp.exp(-0.5 * x * x) * (2.0 * math.pi) ** (-0.5)
+        hid[:, pl.ds(pl.multiple_of(t * block, LANES), block)] = (linear_ref[t] * incline).astype(BF16)
+        full[...] += dot((x * cdf).astype(BF16), gathered(t))
+        return carry
+
+    lax.fori_loop(0, line - 1, early, 0)
+    for t in range(2, near_line):
+        weight_event(t)
+        weight_turn(t)
+    weight_far_event(0, True)
+    for t in range(1, near_line):
+        weight_far_event(t, False)
+    for t in range(3, line):
+        token_event(t)
     for r in range(1, n):
         pre_copy(r).wait()
     own_pre.wait()
-
-    def tokens(d, carry):
-        low = jnp.where(d <= a, a - d, d)
-        flip = line - 1 - a
-        high = line - 1 - jnp.where(d <= flip, flip - d, d)
-        t = jnp.where(side == 0, low, high)
-        m_arrived(t * SIDES + 1 - b)
-
-        def gather(o, total):
-            return total + dot(pre_got[o], landing(o, t))
-
-        x = lax.fori_loop(0, n, gather, jnp.zeros((mine, block), F32))
-        cdf = 0.5 * (1.0 + lax.erf(x * 0.5**0.5))
-        incline = cdf + x * jnp.exp(-0.5 * x * x) * (2.0 * math.pi) ** (-0.5)
-        rows = jnp.concatenate([mall[t * SIDES + i] for i in range(SIDES)], axis=0)
-        hid[t] = (dot(w_ref[...].reshape(mine, width), rows, NT) * incline).astype(BF16)
-        full[...] += dot((x * cdf).astype(BF16), rows)
-        slotted[...] += dot(landing(me, t), rows).astype(BF16)
-        return carry
-
-    lax.fori_loop(0, line, tokens, 0)
+    lax.fori_loop(0, line - 1, late, 0)
+    for t in range(1, near_line):
+        weight_side_event(t)
+    early(line - 1, 0)
+    late(line - 1, 0)
+
 
     piece = width // replicas
     for d in range(replicas):
@@ -505,10 +533,8 @@
         core_copy(x).start()
 
     def outgoing(i, carry):
-        def gather(t, total):
-            return total + dot(hid[t], landing(side * near + i, t), NT)
-
-        hid_out[i] = lax.fori_loop(0, line, gather, jnp.zeros((mine, slots), F32)).astype(BF16)
+        spots = jnp.concatenate([landing(side * near + i, t) for t in range(line)], axis=1)
+        hid_out[i] = dot(hid[...], spots, NT).astype(BF16)
         return carry
 
     lax.fori_loop(0, near, outgoing, 0)
@@ -527,10 +553,6 @@
     groups = next(g for g in range(near_line, 0, -1) if near_line % g == 0 and units // 2 // g % LANES == 0)
     run, each = near // groups, units // 2 // groups
 
-    def h_copy(g, start):
-        over = pl.ds(pl.multiple_of(start + g * each, LANES), each)
-        return pltpu.make_async_copy(h_ref.at[:, over], h_hbm.at[:, over], out_sem.at[3])
-
     def linear(g, carry):
         if shared:
 
@@ -546,6 +568,8 @@
         h_ref[:, to] = (dot(slotted[...], weight, NT) * slope[:, over]).astype(BF16)
         return carry
 
+    for t in range(1, near_line):
+        weight_far_event(t, True)
     lax.fori_loop(0, groups, linear, 0)
 
     own_hidden.wait()
@@ -666,12 +690,13 @@
             pltpu.VMEM((slots, units), BF16),
             pltpu.VMEM((slots, units // 2), F32),
             pltpu.VMEM((units, slots), BF16),
-            pltpu.VMEM((n, mine, slots), BF16),
+            pltpu.VMEM((mine, n * slots), BF16),
             pltpu.VMEM((near, parts, mine // parts, width), BF16),
             pltpu.VMEM((parts, mine // parts, width), BF16),
             pltpu.VMEM((line, 8, block), F32),
             pltpu.VMEM((slots, width), BF16),
-            pltpu.VMEM((line, mine, block), BF16),
+            pltpu.VMEM((mine, line * block), BF16),
+            pltpu.VMEM((line, mine, block), F32),
             pltpu.VMEM((near, mine, slots), BF16),
             pltpu.VMEM((near, mine, slots), BF16),
             pltpu.VMEM((slots, units), BF16),

time: 136 us -> 106 us (0.78)
  Pallas kernels: 134 us -> 105 us
    pallas_call x1, Pallas kernels: 131 us -> 101 us  [fused(): pl.pallas_call(functools.partial(fused_kernel, n, replicas), in_specs=[hb...]
where the time goes in v2:
time: 106 us
  Pallas kernels  105 us (99%)
    pallas_call x1, Pallas kernels, fused(): pl.pallas_call(functools.partial(fused_kernel, n, replicas), in_specs=[hb...  101 us
    pallas_call x1, Pallas kernels, fused(): pl.pallas_call(finish_kernel, in_specs=[hbm] * 5, out_specs=[hbm] * 5, ou...  3.32 us

profile of v2, /device:TPU:0, one launch (start us, length us, event | category | flops | bytes accessed | tf_op | source)
XLA Modules:
  0.0 105.8 jit_solution(11398381090958066148)
XLA Ops:
  0.7 0.6 concatenate.3
  1.3 101.2 %fused.1 = (bf16[256,2560]{1,0:T(8,128)(2,1)}, f32[320,448]{1,0:T(8,128)}, bf16[256,1280]{1,0:T(8,128)(2,1)}, bf16[256,1280]{1,0:T(8,128)(2,1)}, bf16[256,1280]{1,0:T(8,128)(2,1)}) custom-call(bf16[128,1792]{1,0:T(8,128)(2,1)} %m_hbm.1, s32[1,128]{1,0:T(1,128)} %bitcast.5, bf16[256,2560]{1,0:T(8,128)(2,1)} %p_hbm.1, bf16[4,80,1792]{2,1,0:T(8,128)(2,1)} %bitcast.3, ...), custom_call_target="tpu_custom_call" | custom-call | tf_op jit(solution)/shard_map/fused/pallas_call | solution.py:682
  102.5 3.3 %finish.1 = (bf16[256,2560]{1,0:T(8,128)(2,1)}, f32[320,448]{1,0:T(8,128)}, bf16[256,1280]{1,0:T(8,128)(2,1)}, bf16[256,1280]{1,0:T(8,128)(2,1)}, bf16[256,1280]{1,0:T(8,128)(2,1)}) custom-call(bf16[256,2560]{1,0:T(8,128)(2,1)} %get-tuple-element.10.refs_0_, f32[320,448]{1,0:T(8,128)} %get-tuple-element.11.refs_1_, ...), custom_call_target="tpu_custom_call" | custom-call | tf_op jit(solution)/shard_map/finish/pallas_call | solution.py:754
  (2 shorter events, 0.0 us)

commit v3 on v2

--- a/solution.py
+++ b/solution.py
@@ -12,6 +12,7 @@
 WIN = 64
 LANES = 128
 SIDES = 2
+CUTS = 2
 F32 = jnp.float32
 BF16 = jnp.bfloat16
 MESH = pl.DeviceIdType.MESH
@@ -35,13 +36,14 @@
     return dot(high, pick) + dot(mid, pick) + dot(low, pick)
 
 
-def rope_tables(pos_ref, freq_ref, c_ref, s_ref):
+def rope_tables(pos_ref, c_ref, s_ref):
     count = pos_ref.shape[1]
     half, quarter = HEAD // 2, HEAD // 4
     unit = lax.broadcasted_iota(jnp.int32, (LANES, count), 0)
     rows = pos_ref[0:1, :].astype(F32)
     cols = pos_ref[1:2, :].astype(F32)
-    freq = jnp.transpose(jnp.broadcast_to(freq_ref[...], (count, LANES)))
+    rank = (unit % half % quarter).astype(F32)
+    freq = jnp.exp(rank * (-4.0 / HEAD * math.log(10000.0)))
     angles = jnp.where(unit % half < quarter, rows, cols) * freq
     c_ref[...] = jnp.transpose(jnp.cos(angles))
     s_ref[...] = jnp.transpose(jnp.where(unit < half, -1.0, 1.0) * jnp.sin(angles))
@@ -119,7 +121,6 @@
     v_hbm,
     g_hbm,
     pos_ref,
-    freq_ref,
     h_hbm,
     wg_hbm,
     dq_hbm,
@@ -137,12 +138,14 @@
     slotted,
     hid,
     linear_ref,
+    act_ref,
     hid_out,
     hid_got,
     h_ref,
     full,
     part,
     core_got,
+    x_out,
     x_got,
     wg_ref,
     q_ref,
@@ -196,7 +199,7 @@
     here = me % near
     mirror = (me + near) % n
     partner = rep // 2 * 2 + 1 - rep % 2
-    core = rep % 2
+    core, place = rep % 2, rep // 2
     q_own = rep if shared else 0
     q_far = (rep + 2) % replicas if shared else 0
 
@@ -252,20 +255,25 @@
             hid_out.at[to], hid_got.at[here], h_send.at[r - 1], h_recv.at[r - 1], ctx=side * near + to
         )
 
-    def up_copy(t, ref):
+    def cut(h):
+        return pl.ds(h * (rows_here // CUTS), rows_here // CUTS)
+
+    def up_copy(t, ref, h):
         at = (a - t) * SIDES + b
-        return send(ref, mall.at[at], up_sem.at[t], m_recv.at[at], ctx=me + SIDES)
-
-    def down_copy(t, ref):
+        return send(ref.at[cut(h)], mall.at[at, cut(h)], up_sem.at[t, h], m_recv.at[at, h], ctx=me + SIDES)
+
+    def down_copy(t, ref, h):
         at = (a + t) * SIDES + b
-        return send(ref, mall.at[at], down_sem.at[t], m_recv.at[at], ctx=me - SIDES)
-
-    def side_copy(at, ref):
+        return send(ref.at[cut(h)], mall.at[at, cut(h)], down_sem.at[t, h], m_recv.at[at, h], ctx=me - SIDES)
+
+    def side_copy(at, ref, h):
         src = at * SIDES + b
-        return send(ref, mall.at[src], side_sem.at[at], m_recv.at[src], ctx=a * SIDES + 1 - b)
-
-    def m_arrived(src):
-        send(mall.at[src], mall.at[src], up_sem.at[0], m_recv.at[src], ctx=a * SIDES + 1 - b).wait_recv()
+        to = a * SIDES + 1 - b
+        return send(ref.at[cut(h)], mall.at[src, cut(h)], side_sem.at[at, h], m_recv.at[src, h], ctx=to)
+
+    def m_arrived(src, h):
+        ref = mall.at[src, cut(h)]
+        send(ref, ref, up_sem.at[0, 0], m_recv.at[src, h], ctx=a * SIDES + 1 - b).wait_recv()
 
     def mirror_copy():
         return send(
@@ -307,16 +315,17 @@
 
     def x_copy(r):
         peer = (rep + 2 * r) % replicas
-        return send(part.at[peer], x_got.at[r - 1], x_send.at[r - 1], x_recv.at[r - 1], dp=peer)
+        return send(x_out.at[r - 1], x_got.at[r - 1], x_send.at[r - 1], x_recv.at[r - 1], dp=peer)
 
     def when(condition, body):
         pl.when(condition)(body)
 
     for r in range(1, n):
         owner_copy(r).start()
-    when(a + 1 < line, lambda: up_copy(0, m_hbm).start())
-    when(a > 0, lambda: down_copy(0, m_hbm).start())
-    side_copy(a, m_hbm).start()
+    for h in range(CUTS):
+        when(a + 1 < line, lambda h=h: up_copy(0, m_hbm, h).start())
+        when(a > 0, lambda h=h: down_copy(0, m_hbm, h).start())
+        side_copy(a, m_hbm, h).start()
     mirror_copy().start()
 
     locals_[0].wait()
@@ -329,7 +338,7 @@
     lax.fori_loop(0, units // LANES, turn, 0)
     own_pre = pltpu.make_async_copy(unit_rows(me), pre_place(), local_sem.at[8])
     own_pre.start()
-    rope_tables(pos_ref, freq_ref, c_ref, s_ref)
+    rope_tables(pos_ref, c_ref, s_ref)
     full[...] = jnp.zeros_like(full)
     slotted[...] = jnp.zeros_like(slotted)
     for copy in locals_[1:5]:
@@ -350,12 +359,13 @@
         def body(at, below):
             src = at * SIDES + b
             ref = mall.at[src]
-            m_arrived(src)
-            if below:
-                when(a + 1 < line, lambda: up_copy(t, ref).start())
-            else:
-                when(a > 0, lambda: down_copy(t, ref).start())
-            side_copy(at, ref).start()
+            for h in range(CUTS):
+                m_arrived(src, h)
+                if below:
+                    when(a + 1 < line, lambda h=h: up_copy(t, ref, h).start())
+                else:
+                    when(a > 0, lambda h=h: down_copy(t, ref, h).start())
+                side_copy(at, ref, h).start()
 
         both(t, a, line, body)
 
@@ -481,24 +491,33 @@
     def gathered(t):
         return jnp.concatenate([mall[t * SIDES + i] for i in range(SIDES)], axis=0)
 
+    def slotting(t, rows):
+        slotted[...] += dot(landing(me, t), rows).astype(BF16)
+
     def early(d, carry):
         t = nth(d)
-        m_arrived(t * SIDES + 1 - b)
+        for h in range(CUTS):
+            m_arrived(t * SIDES + 1 - b, h)
         rows = gathered(t)
         linear_ref[t] = dot(w_ref[...].reshape(mine, width), rows, NT)
-        slotted[...] += dot(landing(me, t), rows).astype(BF16)
-        return carry
-
-
-    def late(d, carry):
-        t = nth(d)
-
+        slotting(t, rows)
+        return carry
+
+    def activation(t):
         spots = jnp.concatenate([landing(jnp.int32(o), t) for o in range(n)], axis=0)
         x = dot(pre_got[...], spots)
         cdf = 0.5 * (1.0 + lax.erf(x * 0.5**0.5))
         incline = cdf + x * jnp.exp(-0.5 * x * x) * (2.0 * math.pi) ** (-0.5)
-        hid[:, pl.ds(pl.multiple_of(t * block, LANES), block)] = (linear_ref[t] * incline).astype(BF16)
-        full[...] += dot((x * cdf).astype(BF16), gathered(t))
+        return (x * cdf).astype(BF16), incline
+
+    def hid_place(t):
+        return pl.ds(pl.multiple_of(t * block, LANES), block)
+
+    def late(d, carry):
+        t = nth(d)
+        act, incline = activation(t)
+        hid[:, hid_place(t)] = (linear_ref[t] * incline).astype(BF16)
+        full[...] += dot(act, gathered(t))
         return carry
 
     lax.fori_loop(0, line - 1, early, 0)
@@ -510,17 +529,21 @@
         weight_far_event(t, False)
     for t in range(3, line):
         token_event(t)
+    for t in range(1, near_line):
+        weight_side_event(t)
     for r in range(1, n):
         pre_copy(r).wait()
     own_pre.wait()
     lax.fori_loop(0, line - 1, late, 0)
-    for t in range(1, near_line):
-        weight_side_event(t)
-    early(line - 1, 0)
-    late(line - 1, 0)
+    last = nth(jnp.int32(line - 1))
+    act_ref[...], linear_ref[last] = activation(last)
+    for h in range(CUTS):
+        m_arrived(last * SIDES + 1 - b, h)
+    full[...] += dot(act_ref[...], gathered(last))
 
 
     piece = width // replicas
+    span_out = part.shape[2]
     for d in range(replicas):
         lo = d * piece // LANES * LANES
         hi = -(-(d + 1) * piece // LANES) * LANES
@@ -528,9 +551,38 @@
         value = full[:, lo:hi]
         if shift:
             value = pltpu.roll(value, hi - lo - shift, 1)
-        part[d] = value[:, :piece]
+        part[d] = value[:, :span_out]
     for x in range(chips):
         core_copy(x).start()
+    late_rows = gathered(last)
+    late_linear = dot(w_ref[...].reshape(mine, width), late_rows, NT)
+    hid[:, hid_place(last)] = (late_linear * linear_ref[last]).astype(BF16)
+
+    tight = x_out.shape[1] < mine
+    rest = piece % LANES
+    whole = piece - rest
+    lane = lax.broadcasted_iota(jnp.int32, (mine // 2, LANES), 1)
+
+    def packed(value):
+        if not tight:
+            return value
+        top, low = value[: mine // 2], value[mine // 2 :]
+        low = pltpu.roll(low, rest, 1)
+        seam = jnp.where(lane < rest, top[:, whole:], low[:, :LANES])
+        return jnp.concatenate([top[:, :whole], seam, low[:, LANES:]], axis=1)
+
+    def unpacked(value):
+        if not tight:
+            return value
+        low = pltpu.roll(value[:, whole:], span_out - rest, 1)
+        return jnp.concatenate([value[:, :span_out], low], axis=0)
+
+    for x in range(chips):
+        core_copy(x).wait()
+    for r in range(1, chips):
+        x = (place + r) % chips
+        x_out[r - 1] = packed(part[2 * x + core] + core_got[x]).astype(x_out.dtype)
+        x_copy(r).start()
 
     def outgoing(i, carry):
         spots = jnp.concatenate([landing(side * near + i, t) for t in range(line)], axis=1)
@@ -543,12 +595,6 @@
     own_hidden = pltpu.make_async_copy(hid_out.at[here], hid_got.at[here], local_sem.at[9])
     own_hidden.start()
 
-    for x in range(chips):
-        core_copy(x).wait()
-    for x in range(chips):
-        part[2 * x + core] = part[2 * x + core] + core_got[x]
-    for r in range(1, chips):
-        x_copy(r).start()
 
     groups = next(g for g in range(near_line, 0, -1) if near_line % g == 0 and units // 2 // g % LANES == 0)
     run, each = near // groups, units // 2 // groups
@@ -568,6 +614,7 @@
         h_ref[:, to] = (dot(slotted[...], weight, NT) * slope[:, over]).astype(BF16)
         return carry
 
+    slotting(last, gathered(last))
     for t in range(1, near_line):
         weight_far_event(t, True)
     lax.fori_loop(0, groups, linear, 0)
@@ -590,24 +637,26 @@
     outs.append(pltpu.make_async_copy(h_ref, h_hbm, out_sem.at[3]))
     outs[-1].start()
 
-    total = part[rep]
+    total = part[rep] + core_got[place]
     for r in range(1, chips):
         x_copy(r).wait()
-        total = total + x_got[r - 1]
-    wg_ref[...] = total * (rows_here * n * replicas) ** (-0.5)
+        total = total + unpacked(x_got[r - 1].astype(F32))
+    wg_ref[...] = total[:, :piece] * (rows_here * n * replicas) ** (-0.5)
     outs.append(pltpu.make_async_copy(wg_ref, wg_hbm, out_sem.at[4]))
     outs[-1].start()
 
     def sent(t, carry):
-        @pl.when((a - t >= 0) & (a + 1 < line))
-        def _():
-            up_copy(t, mall.at[me]).wait_send()
-
-        @pl.when((a + t < line) & (a > 0))
-        def _():
-            down_copy(t, mall.at[me]).wait_send()
-
-        side_copy(t, mall.at[me]).wait_send()
+        for h in range(CUTS):
+
+            @pl.when((a - t >= 0) & (a + 1 < line))
+            def _():
+                up_copy(t, mall.at[me], h).wait_send()
+
+            @pl.when((a + t < line) & (a > 0))
+            def _():
+                down_copy(t, mall.at[me], h).wait_send()
+
+            side_copy(t, mall.at[me], h).wait_send()
         return carry
 
     lax.fori_loop(0, line, sent, 0)
@@ -664,10 +713,10 @@
     block = SIDES * rows_here
     piece = width // replicas
     chips = replicas // 2
+    span_out = -(-piece // LANES) * LANES
+    tight = piece % LANES * 2 == LANES and mine % 32 == 0
+    across = (mine // 2, 2 * piece) if tight else (mine, span_out)
     parts = replicas if chips == 2 and mine % (16 * replicas) == 0 else 1
-    quarter = HEAD // 4
-    freq = 1.0 / 10000.0 ** (jnp.arange(quarter, dtype=F32) * (4.0 / HEAD))
-    freq = jnp.concatenate([freq] * 4 + [jnp.zeros((LANES - HEAD,), F32)]).reshape(1, LANES)
     vmem = pl.BlockSpec(memory_space=pltpu.VMEM)
     hbm = pl.BlockSpec(memory_space=pl.ANY)
     dma = pltpu.SemaphoreType.DMA
@@ -681,7 +730,7 @@
     ]
     results = pl.pallas_call(
         functools.partial(fused_kernel, n, replicas),
-        in_specs=[hbm, vmem] + [hbm] * 6 + [vmem] * 2,
+        in_specs=[hbm, vmem] + [hbm] * 6 + [vmem],
         out_specs=[hbm] * 5,
         out_shape=shapes,
         scratch_shapes=[
@@ -697,23 +746,25 @@
             pltpu.VMEM((slots, width), BF16),
             pltpu.VMEM((mine, line * block), BF16),
             pltpu.VMEM((line, mine, block), F32),
+            pltpu.VMEM((mine, block), BF16),
             pltpu.VMEM((near, mine, slots), BF16),
             pltpu.VMEM((near, mine, slots), BF16),
             pltpu.VMEM((slots, units), BF16),
             pltpu.VMEM((mine, width), F32),
-            pltpu.VMEM((replicas, mine, piece), F32),
-            pltpu.VMEM((chips, mine, piece), F32),
-            pltpu.VMEM((max(chips - 1, 1), mine, piece), F32),
+            pltpu.VMEM((replicas, mine, span_out), F32),
+            pltpu.VMEM((chips, mine, span_out), F32),
+            pltpu.VMEM((max(chips - 1, 1), *across), F32),
+            pltpu.VMEM((max(chips - 1, 1), *across), F32),
             pltpu.VMEM((mine, piece), F32),
         ]
         + [pltpu.VMEM(query.shape, BF16)] * 7
         + [
             pltpu.VMEM((query.shape[0], LANES), F32),
             pltpu.VMEM((query.shape[0], LANES), F32),
-            dma((n,)),
-            dma((line,)),
-            dma((line,)),
-            dma((line,)),
+            dma((n, CUTS)),
+            dma((line, CUTS)),
+            dma((line, CUTS)),
+            dma((line, CUTS)),
             dma((n - 1,)),
             dma((n - 1,)),
             dma((n - 1,)),
@@ -748,7 +799,6 @@
         value_states,
         out_grad,
         position,
-        freq,
     )
     return tuple(
         pl.pallas_call(

time: 106 us -> 103 us (0.972)
  Pallas kernels: 105 us -> 102 us
    pallas_call x1, Pallas kernels: 101 us -> 98.4 us  [fused(): pl.pallas_call(functools.partial(fused_kernel, n, replicas), in_specs=[hb...]
where the time goes in v3:
time: 103 us; the launch traced here: 102 us
  Pallas kernels  102 us (99%)
    pallas_call x1, Pallas kernels, fused(): pl.pallas_call(functools.partial(fused_kernel, n, replicas), in_specs=[hb...  98.4 us
    pallas_call x1, Pallas kernels, fused(): pl.pallas_call(finish_kernel, in_specs=[hbm] * 5, out_specs=[hbm] * 5, ou...  3.32 us

profile of v3, /device:TPU:0, one launch (start us, length us, event | category | flops | bytes accessed | tf_op | source)
XLA Modules:
  0.0 102.4 jit_solution(7179046627112706621)
XLA Ops:
  0.6 98.4 %fused.1 = (bf16[256,2560]{1,0:T(8,128)(2,1)}, f32[320,448]{1,0:T(8,128)}, bf16[256,1280]{1,0:T(8,128)(2,1)}, bf16[256,1280]{1,0:T(8,128)(2,1)}, bf16[256,1280]{1,0:T(8,128)(2,1)}) custom-call(bf16[128,1792]{1,0:T(8,128)(2,1)} %m_hbm.1, s32[1,128]{1,0:T(1,128)} %bitcast.3, bf16[256,2560]{1,0:T(8,128)(2,1)} %p_hbm.1, bf16[4,80,1792]{2,1,0:T(8,128)(2,1)} %bitcast.2, ...), custom_call_target="tpu_custom_call" | custom-call | tf_op jit(solution)/shard_map/fused/pallas_call | solution.py:731
  99.1 3.3 %finish.1 = (bf16[256,2560]{1,0:T(8,128)(2,1)}, f32[320,448]{1,0:T(8,128)}, bf16[256,1280]{1,0:T(8,128)(2,1)}, bf16[256,1280]{1,0:T(8,128)(2,1)}, bf16[256,1280]{1,0:T(8,128)(2,1)}) custom-call(bf16[256,2560]{1,0:T(8,128)(2,1)} %get-tuple-element.10.refs_0_, f32[320,448]{1,0:T(8,128)} %get-tuple-element.11.refs_1_, ...), custom_call_target="tpu_custom_call" | custom-call | tf_op jit(solution)/shard_map/finish/pallas_call | solution.py:804

commit v4 on v3

--- a/solution.py
+++ b/solution.py
@@ -121,11 +121,11 @@
     v_hbm,
     g_hbm,
     pos_ref,
-    h_hbm,
-    wg_hbm,
-    dq_hbm,
-    dk_hbm,
-    dv_hbm,
+    h_ref,
+    wg_ref,
+    dq_ref,
+    dk_ref,
+    dv_ref,
     mall,
     owners,
     pre,
@@ -135,26 +135,22 @@
     fall,
     w_ref,
     code,
+    ranks,
     slotted,
     hid,
     linear_ref,
     act_ref,
     hid_out,
     hid_got,
-    h_ref,
     full,
     part,
     core_got,
     x_out,
     x_got,
-    wg_ref,
     q_ref,
     k_ref,
     v_ref,
     g_ref,
-    dq_ref,
-    dk_ref,
-    dv_ref,
     c_ref,
     s_ref,
     m_recv,
@@ -179,7 +175,6 @@
     x_send,
     x_recv,
     local_sem,
-    out_sem,
 ):
     line = n // SIDES
     near = n // 2
@@ -249,10 +244,21 @@
         peer = (me + r) % n
         return send(unit_rows(peer), pre_place(), p_send.at[r - 1], p_recv.at[r - 1], ctx=peer)
 
-    def hidden_copy(r):
+    def turn_side(phase):
+        return side if phase == 0 else 1 - side
+
+    def half_lanes(phase):
+        return pl.ds(pl.multiple_of(turn_side(phase) * (slots // 2), LANES), slots // 2)
+
+    def hidden_copy(r, phase):
         to = (here + r) % near
+        lanes = half_lanes(phase)
         return send(
-            hid_out.at[to], hid_got.at[here], h_send.at[r - 1], h_recv.at[r - 1], ctx=side * near + to
+            hid_out.at[to, :, lanes],
+            hid_got.at[here, :, lanes],
+            h_send.at[r - 1, phase],
+            h_recv.at[r - 1, phase],
+            ctx=side * near + to,
         )
 
     def cut(h):
@@ -438,14 +444,6 @@
         return carry
 
     lax.fori_loop(0, steps, attend, 0)
-    outs = [
-        pltpu.make_async_copy(dq_ref, dq_hbm, out_sem.at[0]),
-        pltpu.make_async_copy(dk_ref, dk_hbm, out_sem.at[1]),
-        pltpu.make_async_copy(dv_ref, dv_hbm, out_sem.at[2]),
-    ]
-    for copy in outs:
-        copy.start()
-
     far = (1 - side) * (units // 2)
 
     def incline(j, carry):
@@ -469,13 +467,28 @@
     earlier = earlier.astype(F32).astype(BF16)
     names = lax.broadcasted_iota(jnp.int32, (padded, rows_here), 0)
     base = jnp.zeros((padded, 1), F32)
+    cap = slots // n
+    mine_only = lax.broadcasted_iota(jnp.int32, (padded, 1), 0) == me
+    lane_of = lax.broadcasted_iota(jnp.int32, (1, slots), 1)
+    in_source = (lane_of % cap).astype(F32)
+    slot_of = jnp.full((1, slots), -1.0, F32)
     for s in range(n):
         onehot = (names == owners[s]).astype(F32)
-        count = dot(onehot.astype(BF16), earlier) + base
-        position = jnp.sum(onehot * (count + names.astype(F32) * float(slots)), axis=0, keepdims=True)
-        base = base + jnp.sum(onehot, axis=1, keepdims=True)
+        count = dot(onehot.astype(BF16), earlier)
+        named = names.astype(F32)
+        position = jnp.sum(onehot * (count + base + named * float(slots)), axis=0, keepdims=True)
+        ranked = jnp.sum(onehot * (count + named * float(slots // 2)), axis=0, keepdims=True)
+        tally = jnp.sum(onehot, axis=1, keepdims=True)
+        start = jnp.sum(jnp.where(mine_only, base, 0.0), axis=0, keepdims=True)
+        held = jnp.sum(jnp.where(mine_only, tally, 0.0), axis=0, keepdims=True)
+        spot_of = jnp.where(in_source < held, start + in_source, -1.0)
+        slot_of = jnp.where(lane_of // cap == s, spot_of, slot_of)
+        base = base + tally
         lo = s % SIDES * rows_here
         code[s // SIDES, :, lo : lo + rows_here] = jnp.broadcast_to(position, (8, rows_here))
+        ranks[s // SIDES, :, lo : lo + rows_here] = jnp.broadcast_to(
+            ranked + float(s % near * cap), (8, rows_here)
+        )
     standing = lax.broadcasted_iota(jnp.int32, (slots, block), 0).astype(F32)
 
     def landing(o, t):
@@ -509,6 +522,31 @@
         cdf = 0.5 * (1.0 + lax.erf(x * 0.5**0.5))
         incline = cdf + x * jnp.exp(-0.5 * x * x) * (2.0 * math.pi) ** (-0.5)
         return (x * cdf).astype(BF16), incline
+
+    ranking = lax.broadcasted_iota(jnp.int32, (slots // 2, block), 0).astype(F32)
+
+    def send_hidden(phase):
+        first = turn_side(phase) * near_line
+        lanes = half_lanes(phase)
+        blocks = pl.ds(pl.multiple_of(first * block, LANES), near_line * block)
+
+        def outgoing(i, carry):
+            shift = ((side * near + i) * (slots // 2)).astype(F32)
+            spots = [ranking == ranks[first + j, 0:1, :] - shift for j in range(near_line)]
+            spots = jnp.concatenate([spot.astype(F32).astype(BF16) for spot in spots], axis=1)
+            hid_out[i, :, lanes] = dot(hid[:, blocks], spots, NT).astype(BF16)
+            return carry
+
+        lax.fori_loop(0, near, outgoing, 0)
+        for r in range(1, near):
+            hidden_copy(r, phase).start()
+        own_hidden(phase).start()
+
+    def own_hidden(phase):
+        lanes = half_lanes(phase)
+        return pltpu.make_async_copy(
+            hid_out.at[here, :, lanes], hid_got.at[here, :, lanes], local_sem.at[9 + phase]
+        )
 
     def hid_place(t):
         return pl.ds(pl.multiple_of(t * block, LANES), block)
@@ -534,7 +572,9 @@
     for r in range(1, n):
         pre_copy(r).wait()
     own_pre.wait()
-    lax.fori_loop(0, line - 1, late, 0)
+    lax.fori_loop(0, near_line, late, 0)
+    send_hidden(0)
+    lax.fori_loop(near_line, line - 1, late, 0)
     last = nth(jnp.int32(line - 1))
     act_ref[...], linear_ref[last] = activation(last)
     for h in range(CUTS):
@@ -584,16 +624,7 @@
         x_out[r - 1] = packed(part[2 * x + core] + core_got[x]).astype(x_out.dtype)
         x_copy(r).start()
 
-    def outgoing(i, carry):
-        spots = jnp.concatenate([landing(side * near + i, t) for t in range(line)], axis=1)
-        hid_out[i] = dot(hid[...], spots, NT).astype(BF16)
-        return carry
-
-    lax.fori_loop(0, near, outgoing, 0)
-    for r in range(1, near):
-        hidden_copy(r).start()
-    own_hidden = pltpu.make_async_copy(hid_out.at[here], hid_got.at[here], local_sem.at[9])
-    own_hidden.start()
+    send_hidden(1)
 
 
     groups = next(g for g in range(near_line, 0, -1) if near_line % g == 0 and units // 2 // g % LANES == 0)
@@ -619,12 +650,11 @@
         weight_far_event(t, True)
     lax.fori_loop(0, groups, linear, 0)
 
-    own_hidden.wait()
-    for r in range(1, near):
-        hidden_copy(r).wait()
-    spot = lax.broadcasted_iota(jnp.int32, (slots, slots), 0) == lax.broadcasted_iota(
-        jnp.int32, (slots, slots), 1
-    )
+    for phase in range(2):
+        own_hidden(phase).wait()
+        for r in range(1, near):
+            hidden_copy(r, phase).wait()
+    spot = lax.broadcasted_iota(jnp.int32, (slots, slots), 0).astype(F32) == slot_of
     spot = spot.astype(F32).astype(BF16)
 
     def settle(g, carry):
@@ -634,16 +664,12 @@
         return carry
 
     lax.fori_loop(0, groups, settle, 0)
-    outs.append(pltpu.make_async_copy(h_ref, h_hbm, out_sem.at[3]))
-    outs[-1].start()
 
     total = part[rep] + core_got[place]
     for r in range(1, chips):
         x_copy(r).wait()
         total = total + unpacked(x_got[r - 1].astype(F32))
     wg_ref[...] = total[:, :piece] * (rows_here * n * replicas) ** (-0.5)
-    outs.append(pltpu.make_async_copy(wg_ref, wg_hbm, out_sem.at[4]))
-    outs[-1].start()
 
     def sent(t, carry):
         for h in range(CUTS):
@@ -684,21 +710,14 @@
             return carry
 
         lax.fori_loop(0, near, passed, 0)
-    for copy in outs:
-        copy.wait()
 
 
 def finish_kernel(*refs):
-    ins, outs, held = refs[:5], refs[5:10], refs[10:15]
-    in_sem, out_sem = refs[15:]
-    first = [pltpu.make_async_copy(ins[i], held[i], in_sem.at[i]) for i in range(5)]
-    second = [pltpu.make_async_copy(held[i], outs[i], out_sem.at[i]) for i in range(5)]
-    for copy in first:
+    count = len(refs) // 2
+    copies = [pltpu.make_async_copy(refs[i], refs[count + i], refs[-1].at[i]) for i in range(count)]
+    for copy in copies:
         copy.start()
-    for i in range(5):
-        first[i].wait()
-        second[i].start()
-    for copy in second:
+    for copy in copies:
         copy.wait()
 
 
@@ -731,8 +750,8 @@
     results = pl.pallas_call(
         functools.partial(fused_kernel, n, replicas),
         in_specs=[hbm, vmem] + [hbm] * 6 + [vmem],
-        out_specs=[hbm] * 5,
-        out_shape=shapes,
+        out_specs=[vmem] * 5,
+        out_shape=[pltpu.VMEM(shape.shape, shape.dtype) for shape in shapes],
         scratch_shapes=[
             pltpu.VMEM((n, rows_here, width), BF16),
             pltpu.VMEM((n, 1, rows_here), jnp.int32),
@@ -743,21 +762,20 @@
             pltpu.VMEM((near, parts, mine // parts, width), BF16),
             pltpu.VMEM((parts, mine // parts, width), BF16),
             pltpu.VMEM((line, 8, block), F32),
+            pltpu.VMEM((line, 8, block), F32),
             pltpu.VMEM((slots, width), BF16),
             pltpu.VMEM((mine, line * block), BF16),
             pltpu.VMEM((line, mine, block), F32),
             pltpu.VMEM((mine, block), BF16),
             pltpu.VMEM((near, mine, slots), BF16),
             pltpu.VMEM((near, mine, slots), BF16),
-            pltpu.VMEM((slots, units), BF16),
             pltpu.VMEM((mine, width), F32),
             pltpu.VMEM((replicas, mine, span_out), F32),
             pltpu.VMEM((chips, mine, span_out), F32),
-            pltpu.VMEM((max(chips - 1, 1), *across), F32),
-            pltpu.VMEM((max(chips - 1, 1), *across), F32),
-            pltpu.VMEM((mine, piece), F32),
+            pltpu.VMEM((max(chips - 1, 1), *across), BF16),
+            pltpu.VMEM((max(chips - 1, 1), *across), BF16),
         ]
-        + [pltpu.VMEM(query.shape, BF16)] * 7
+        + [pltpu.VMEM(query.shape, BF16)] * 4
         + [
             pltpu.VMEM((query.shape[0], LANES), F32),
             pltpu.VMEM((query.shape[0], LANES), F32),
@@ -776,14 +794,13 @@
             dma((near_line,)),
             dma((near,)),
             dma((near, 2)),
-            dma((near - 1,)),
-            dma((near - 1,)),
+            dma((near - 1, 2)),
+            dma((near - 1, 2)),
             dma((chips,)),
             dma((chips,)),
             dma((max(chips - 1, 1),)),
             dma((max(chips - 1, 1),)),
-            dma((10,)),
-            dma((5,)),
+            dma((11,)),
         ],
         compiler_params=pltpu.CompilerParams(
             collective_id=0, has_side_effects=True, vmem_limit_bytes=60 * 2**20
@@ -803,10 +820,11 @@
     return tuple(
         pl.pallas_call(
             finish_kernel,
-            in_specs=[hbm] * 5,
+            in_specs=[vmem] * 5,
             out_specs=[hbm] * 5,
             out_shape=shapes,
-            scratch_shapes=[pltpu.VMEM(shape.shape, shape.dtype) for shape in shapes] + [dma((5,)), dma((5,))],
+            scratch_shapes=[dma((5,))],
+            compiler_params=pltpu.CompilerParams(vmem_limit_bytes=2**20),
             name="finish",
         )(*results)
     )

time: 103 us -> 95.3 us (0.925)
  Pallas kernels: 102 us -> 94.5 us
    pallas_call x1, Pallas kernels: 98.4 us -> 92.5 us  [fused(): pl.pallas_call(functools.partial(fused_kernel, n, replicas), in_specs=[hb...]
    pallas_call x1, Pallas kernels: 3.32 us -> 1.96 us  [fused(): pl.pallas_call(finish_kernel, in_specs=[vmem] * 5, out_specs=[hbm] * 5, o...]
where the time goes in v4:
time: 95.3 us; the launch traced here: 95.1 us
  Pallas kernels  94.5 us (99%)
    pallas_call x1, Pallas kernels, fused(): pl.pallas_call(functools.partial(fused_kernel, n, replicas), in_specs=[hb...  92.5 us
    pallas_call x1, Pallas kernels, fused(): pl.pallas_call(finish_kernel, in_specs=[vmem] * 5, out_specs=[hbm] * 5, o...  1.96 us

profile of v4, /device:TPU:0, one launch (start us, length us, event | category | flops | bytes accessed | tf_op | source)
XLA Modules:
  0.0 95.1 jit_solution(6920019754409242858)
XLA Ops:
  0.6 92.5 %fused.1 = (bf16[256,2560]{1,0:T(8,128)(2,1)S(1)}, f32[320,448]{1,0:T(8,128)S(1)}, bf16[256,1280]{1,0:T(8,128)(2,1)S(1)}, bf16[256,1280]{1,0:T(8,128)(2,1)S(1)}, bf16[256,1280]{1,0:T(8,128)(2,1)S(1)}) custom-call(bf16[128,1792]{1,0:T(8,128)(2,1)} %m_hbm.1, s32[1,128]{1,0:T(1,128)} %bitcast.3, bf16[256,2560]{1,0:T(8,128)(2,1)} %p_hbm.1, ...), custom_call_target="tpu_custom_call" | custom-call | tf_op jit(solution)/shard_map/fused/pallas_call | solution.py:750
  93.2 2.0 %finish.1 = (bf16[256,2560]{1,0:T(8,128)(2,1)}, f32[320,448]{1,0:T(8,128)}, bf16[256,1280]{1,0:T(8,128)(2,1)}, bf16[256,1280]{1,0:T(8,128)(2,1)}, bf16[256,1280]{1,0:T(8,128)(2,1)}) custom-call(bf16[256,2560]{1,0:T(8,128)(2,1)S(1)} %get-tuple-element.10.refs_0_, f32[320,448]{1,0:T(8,128)S(1)} %get-tuple-element.11.refs_1_, ...), custom_call_target="tpu_custom_call" | custom-call | tf_op jit(solution)/shard_map/finish/pallas_call | solution.py:821

commit v5 on v4

--- a/solution.py
+++ b/solution.py
@@ -373,7 +373,9 @@
                     when(a > 0, lambda h=h: down_copy(t, ref, h).start())
                 side_copy(at, ref, h).start()
 
-        both(t, a, line, body)
+        when((side == 1) & (a + t < line), lambda: body(a + t, False))
+        when(a - t >= 0, lambda: body(a - t, True))
+        when((side == 0) & (a + t < line), lambda: body(a + t, False))
 
     def across(src):
         if shared:
@@ -419,8 +421,8 @@
         (1, event(token_event, 1)),
         (2, event(weight_event, 0)),
         (2, event(weight_turn, 0)),
-        (4, event(token_event, 2)),
-        (4, send_pre),
+        (3, event(token_event, 2)),
+        (3, send_pre),
         (5, event(weight_side_event, 0)),
         (6, event(weight_event, 1)),
         (6, event(weight_turn, 1)),
@@ -567,12 +569,12 @@
         weight_far_event(t, False)
     for t in range(3, line):
         token_event(t)
-    for t in range(1, near_line):
-        weight_side_event(t)
     for r in range(1, n):
         pre_copy(r).wait()
     own_pre.wait()
     lax.fori_loop(0, near_line, late, 0)
+    for t in range(1, near_line):
+        weight_side_event(t)
     send_hidden(0)
     lax.fori_loop(near_line, line - 1, late, 0)
     last = nth(jnp.int32(line - 1))
@@ -592,11 +594,12 @@
         if shift:
             value = pltpu.roll(value, hi - lo - shift, 1)
         part[d] = value[:, :span_out]
-    for x in range(chips):
-        core_copy(x).start()
+    for r in range(1, chips + 1):
+        core_copy((place + r) % chips).start()
     late_rows = gathered(last)
     late_linear = dot(w_ref[...].reshape(mine, width), late_rows, NT)
     hid[:, hid_place(last)] = (late_linear * linear_ref[last]).astype(BF16)
+    send_hidden(1)
 
     tight = x_out.shape[1] < mine
     rest = piece % LANES
@@ -617,14 +620,11 @@
         low = pltpu.roll(value[:, whole:], span_out - rest, 1)
         return jnp.concatenate([value[:, :span_out], low], axis=0)
 
-    for x in range(chips):
-        core_copy(x).wait()
     for r in range(1, chips):
         x = (place + r) % chips
+        core_copy(x).wait()
         x_out[r - 1] = packed(part[2 * x + core] + core_got[x]).astype(x_out.dtype)
         x_copy(r).start()
-
-    send_hidden(1)
 
 
     groups = next(g for g in range(near_line, 0, -1) if near_line % g == 0 and units // 2 // g % LANES == 0)
@@ -665,6 +665,7 @@
 
     lax.fori_loop(0, groups, settle, 0)
 
+    core_copy(place).wait()
     total = part[rep] + core_got[place]
     for r in range(1, chips):
         x_copy(r).wait()

time: 95.3 us -> 92.6 us (0.972)
  Pallas kernels: 94.5 us -> 91.8 us
    pallas_call x1, Pallas kernels: 92.5 us -> 89.8 us  [fused(): pl.pallas_call(functools.partial(fused_kernel, n, replicas), in_specs=[hb...]
where the time goes in v5:
time: 92.6 us; the launch traced here: 92.4 us
  Pallas kernels  91.8 us (99%)
    pallas_call x1, Pallas kernels, fused(): pl.pallas_call(functools.partial(fused_kernel, n, replicas), in_specs=[hb...  89.8 us
    pallas_call x1, Pallas kernels, fused(): pl.pallas_call(finish_kernel, in_specs=[vmem] * 5, out_specs=[hbm] * 5, o...  1.96 us

profile of v5, /device:TPU:0, one launch (start us, length us, event | category | flops | bytes accessed | tf_op | source)
XLA Modules:
  0.0 92.4 jit_solution(15390177540258401384)
XLA Ops:
  0.6 89.8 %fused.1 = (bf16[256,2560]{1,0:T(8,128)(2,1)S(1)}, f32[320,448]{1,0:T(8,128)S(1)}, bf16[256,1280]{1,0:T(8,128)(2,1)S(1)}, bf16[256,1280]{1,0:T(8,128)(2,1)S(1)}, bf16[256,1280]{1,0:T(8,128)(2,1)S(1)}) custom-call(bf16[128,1792]{1,0:T(8,128)(2,1)} %m_hbm.1, s32[1,128]{1,0:T(1,128)} %bitcast.3, bf16[256,2560]{1,0:T(8,128)(2,1)} %p_hbm.1, ...), custom_call_target="tpu_custom_call" | custom-call | tf_op jit(solution)/shard_map/fused/pallas_call | solution.py:751
  90.4 2.0 %finish.1 = (bf16[256,2560]{1,0:T(8,128)(2,1)}, f32[320,448]{1,0:T(8,128)}, bf16[256,1280]{1,0:T(8,128)(2,1)}, bf16[256,1280]{1,0:T(8,128)(2,1)}, bf16[256,1280]{1,0:T(8,128)(2,1)}) custom-call(bf16[256,2560]{1,0:T(8,128)(2,1)S(1)} %get-tuple-element.10.refs_0_, f32[320,448]{1,0:T(8,128)S(1)} %get-tuple-element.11.refs_1_, ...), custom_call_target="tpu_custom_call" | custom-call | tf_op jit(solution)/shard_map/finish/pallas_call | solution.py:822

commit v6 on v5

--- a/solution.py
+++ b/solution.py
@@ -423,9 +423,9 @@
         (2, event(weight_turn, 0)),
         (3, event(token_event, 2)),
         (3, send_pre),
-        (5, event(weight_side_event, 0)),
-        (6, event(weight_event, 1)),
-        (6, event(weight_turn, 1)),
+        (4, event(weight_event, 1)),
+        (4, event(weight_turn, 1)),
+        (4, event(weight_side_event, 0)),
         (6, event(weight_far_event, 0, False)),
     ]
 

time: 92.6 us -> 92.6 us (level)
  no operation moved by 1% of the time
where the time goes in v6:
time: 92.6 us; the launch traced here: 92.4 us
  Pallas kernels  91.8 us (99%)
    pallas_call x1, Pallas kernels, fused(): pl.pallas_call(functools.partial(fused_kernel, n, replicas), in_specs=[hb...  89.8 us
    pallas_call x1, Pallas kernels, fused(): pl.pallas_call(finish_kernel, in_specs=[vmem] * 5, out_specs=[hbm] * 5, o...  1.96 us

profile of v6, /device:TPU:0, one launch (start us, length us, event | category | flops | bytes accessed | tf_op | source)
XLA Modules:
  0.0 92.4 jit_solution(18209806746432214861)
XLA Ops:
  0.6 89.8 %fused.1 = (bf16[256,2560]{1,0:T(8,128)(2,1)S(1)}, f32[320,448]{1,0:T(8,128)S(1)}, bf16[256,1280]{1,0:T(8,128)(2,1)S(1)}, bf16[256,1280]{1,0:T(8,128)(2,1)S(1)}, bf16[256,1280]{1,0:T(8,128)(2,1)S(1)}) custom-call(bf16[128,1792]{1,0:T(8,128)(2,1)} %m_hbm.1, s32[1,128]{1,0:T(1,128)} %bitcast.3, bf16[256,2560]{1,0:T(8,128)(2,1)} %p_hbm.1, ...), custom_call_target="tpu_custom_call" | custom-call | tf_op jit(solution)/shard_map/fused/pallas_call | solution.py:751
  90.4 2.0 %finish.1 = (bf16[256,2560]{1,0:T(8,128)(2,1)}, f32[320,448]{1,0:T(8,128)}, bf16[256,1280]{1,0:T(8,128)(2,1)}, bf16[256,1280]{1,0:T(8,128)(2,1)}, bf16[256,1280]{1,0:T(8,128)(2,1)}) custom-call(bf16[256,2560]{1,0:T(8,128)(2,1)S(1)} %get-tuple-element.10.refs_0_, f32[320,448]{1,0:T(8,128)S(1)} %get-tuple-element.11.refs_1_, ...), custom_call_target="tpu_custom_call" | custom-call | tf_op jit(solution)/shard_map/finish/pallas_call | solution.py:822
